TPU v7x, 512 devices: a whole 4x8x8 slice. The times are simulated.
512 devices in a mesh: dp: 32 (over z_lo, y, core), ctx: 16 (over z_hi, x).
Axes of the slice: x: 4, y: 8, z: 8 (z_hi: 4, z_lo: 2; z = z_hi * 2 + z_lo), core: 2. Of those that a mesh axis runs over, the one named last changes fastest.
Arguments:
- output_gradient: float32 [32, 8, 131072], P('dp', None, 'ctx'), may hold values from -6 to 6
- input_spectrum: float32 [32, 8, 2, 131072], P('dp', None, None, 'ctx'), may hold values from -0.013671875 to 0.013671875
- filter_spectrum: float32 [8, 2, 131072], P(None, None, 'ctx'), may hold values from -12 to 12
Outputs:
- input_gradient: float32 [32, 8, 131072], P('dp', None, 'ctx')
- filter_gradient: float32 [8, 2, 131072], P(None, None, ('ctx', 'dp'))
All inputs are finite; a program needn't handle non-finite values.
Results may differ from a plain program's by a relative error of at most 0.0001.
Values sent between devices are 32-bit elements; how exact they have to be, the bound alone decides.
No kernel may reach another device: no remote copies, remote signals or barrier semaphores. Data moves between devices by JAX's collectives and lax.ppermute only.
A program may use at most 128 MiB of HBM per device.

v0:
```python
import math

import jax
import jax.numpy as jnp
from jax import lax
from jax.sharding import PartitionSpec as P

precise = lax.Precision.HIGHEST


def split_up(array, dim, peers):
    lengths = array.shape
    parts = array.reshape(*lengths[:dim], peers, lengths[dim] // peers, *lengths[dim + 1 :])
    return jnp.moveaxis(parts, dim, 0)


def piece_ends(length, count):
    unit = 8 if length >= 8 * count else 1
    return [length // unit * k // count * unit for k in range(1, count)]


def in_order(parts, dim):
    parts = jnp.moveaxis(parts, 0, dim)
    lengths = parts.shape
    return parts.reshape(*lengths[:dim], lengths[dim] * lengths[dim + 1], *lengths[dim + 2 :])


def cut_exchange(array, axis, pieces, split_dim, concat_dim):
    parts = split_up(array, split_dim, lax.axis_size(axis))
    split_at = max(range(1, max(2, parts.ndim - 1)), key=lambda d: parts.shape[d])
    finished = []
    for piece in jnp.split(parts, piece_ends(parts.shape[split_at], pieces), axis=split_at):
        if piece.size:
            finished.append(lax.all_to_all(piece, axis, split_axis=0, concat_axis=0, tiled=True))
    return in_order(jnp.concatenate(finished, axis=split_at), concat_dim)


def sent_and_summed(array, axis, dim):
    peers = lax.axis_size(axis)
    parts = lax.all_to_all(split_up(array, dim, peers), axis, 0, 0, tiled=True)
    return jnp.sum(parts, axis=0)


def rotate(real_part, imag_part, phase):
    cosine = jnp.cos(phase)
    sine = jnp.sin(phase)
    return (real_part * cosine - imag_part * sine, real_part * sine + imag_part * cosine)


def reverse(index, sections):
    result = jnp.zeros_like(index)
    for level in range(sections):
        result = result | (index >> level & 1) << sections - 1 - level
    return result


def square_table(order_size, sign_value):
    series = jnp.arange(order_size, dtype=jnp.int32)
    powers = series[:, None] * series[None, :] % order_size
    phase = sign_value * 2.0 * math.pi / order_size * powers.astype(jnp.float32)
    return (jnp.cos(phase), jnp.sin(phase))


def device_table(axis_size, sign_value):
    sections = axis_size.bit_length() - 1
    series = jnp.arange(axis_size, dtype=jnp.int32)
    powers = reverse(series, sections)[:, None] * series[None, :] % axis_size
    phase = sign_value * 2.0 * math.pi / axis_size * powers.astype(jnp.float32)
    return (jnp.cos(phase), jnp.sin(phase))


def complex_product(form, left_real, left_imag, right_real, right_imag):
    real_out = jnp.einsum(form, left_real, right_real, precision=precise) - jnp.einsum(
        form, left_imag, right_imag, precision=precise
    )
    imag_out = jnp.einsum(form, left_real, right_imag, precision=precise) + jnp.einsum(
        form, left_imag, right_real, precision=precise
    )
    return (real_out, imag_out)


def local_dft(real_part, imag_part, sign_value):
    full_shape = real_part.shape
    length = full_shape[-1]
    inner_size = 1 << (length.bit_length() - 1) // 2
    outer_size = length // inner_size
    real_part = real_part.reshape(-1, outer_size, inner_size)
    imag_part = imag_part.reshape(-1, outer_size, inner_size)
    cos_outer, sin_outer = square_table(outer_size, sign_value)
    first_real, first_imag = complex_product(
        "nk,ska->sna", cos_outer, sin_outer, real_part, imag_part
    )
    series_outer = jnp.arange(outer_size, dtype=jnp.int32)
    series_inner = jnp.arange(inner_size, dtype=jnp.int32)
    powers = series_outer[:, None] * series_inner[None, :]
    first_real, first_imag = rotate(
        first_real, first_imag, sign_value * 2.0 * math.pi / length * powers.astype(jnp.float32)
    )
    cos_inner, sin_inner = square_table(inner_size, sign_value)
    last_real, last_imag = complex_product(
        "ma,sna->smn", cos_inner, sin_inner, first_real, first_imag
    )
    return (last_real.reshape(full_shape), last_imag.reshape(full_shape))


def signals(samples, positions, length):
    phase = -0.5 * math.pi / length * positions.astype(jnp.float32)
    return jnp.stack([samples * jnp.cos(phase), samples * jnp.sin(phase)], axis=2)


def forward_transpose(samples):
    axis_size = lax.axis_size("ctx")
    self_index = lax.axis_index("ctx")
    tokens = samples.shape[-1]
    length = tokens * axis_size
    piece_size = tokens // axis_size
    spread = lax.all_to_all(samples[:, :, None, :], "ctx", split_axis=3, concat_axis=2, tiled=True)
    rows_index = jnp.arange(axis_size, dtype=jnp.int32)[:, None] * tokens
    columns_index = self_index * piece_size + jnp.arange(piece_size, dtype=jnp.int32)[None, :]
    current = signals(spread, rows_index + columns_index, length)
    cos_table, sin_table = device_table(axis_size, -1.0)
    new_real, new_imag = complex_product(
        "qd,bcdt->bcqt", cos_table, sin_table, current[:, :, 0], current[:, :, 1]
    )
    mixed = jnp.stack([new_real, new_imag], axis=2)
    back = lax.all_to_all(mixed, "ctx", split_axis=3, concat_axis=4, tiled=True)
    return back.reshape(back.shape[:3] + (tokens,))


def inverse_transpose(current):
    axis_size = lax.axis_size("ctx")
    tokens = current.shape[-1]
    spread = cut_exchange(current[:, :, :, None, :], "ctx", 2, 4, 3)
    cos_table, sin_table = device_table(axis_size, 1.0)
    new_real, new_imag = complex_product(
        "qd,bcqt->bcdt", cos_table, sin_table, spread[:, :, 0], spread[:, :, 1]
    )
    mixed = jnp.stack([new_real, new_imag], axis=2)
    back = lax.all_to_all(mixed, "ctx", split_axis=3, concat_axis=4, tiled=True)
    return back.reshape(back.shape[:3] + (tokens,))


def per_device(output_gradient, input_spectrum, filter_spectrum):
    axis_size = lax.axis_size("ctx")
    self_index = lax.axis_index("ctx")
    tokens = output_gradient.shape[-1]
    length = tokens * axis_size
    sections = axis_size.bit_length() - 1
    current = forward_transpose(output_gradient)
    series = jnp.arange(tokens, dtype=jnp.int32)
    residue = reverse(self_index, sections)
    phase = -2.0 * math.pi / length * (residue * series).astype(jnp.float32)
    grad_real, grad_imag = rotate(current[:, :, 0], current[:, :, 1], phase)
    grad_real, grad_imag = local_dft(grad_real, grad_imag, -1.0)
    saved_real = input_spectrum[:, :, 0]
    saved_imag = input_spectrum[:, :, 1]
    term_real = jnp.sum(grad_real * saved_real + grad_imag * saved_imag, axis=0)
    term_imag = jnp.sum(grad_imag * saved_real - grad_real * saved_imag, axis=0)
    filter_gradient = sent_and_summed(jnp.stack([term_real, term_imag], axis=1), "dp", 2)
    filter_real = filter_spectrum[:, 0]
    filter_imag = filter_spectrum[:, 1]
    prod_real = grad_real * filter_real + grad_imag * filter_imag
    prod_imag = grad_imag * filter_real - grad_real * filter_imag
    prod_real, prod_imag = local_dft(prod_real, prod_imag, 1.0)
    prod_real, prod_imag = rotate(prod_real, prod_imag, -phase)
    current = jnp.stack([prod_real, prod_imag], axis=2)
    current = inverse_transpose(current)
    positions = self_index * tokens + series
    phase_back = 0.5 * math.pi / length * positions.astype(jnp.float32)
    turned = current[:, :, 0] * jnp.cos(phase_back) - current[:, :, 1] * jnp.sin(phase_back)
    input_gradient = turned / length
    return (input_gradient, filter_gradient)


def solution(mesh):
    in_specs = (P("dp", None, "ctx"), P("dp", None, None, "ctx"), P(None, None, "ctx"))
    out_specs = (P("dp", None, "ctx"), P(None, None, ("ctx", "dp")))
    return jax.shard_map(
        per_device, mesh=mesh, in_specs=in_specs, out_specs=out_specs, check_vma=False
    )
```

profile of v0, /device:TPU:8, one launch (start us, length us, event | category | flops | bytes accessed | tf_op | source)
XLA Modules:
  0.0 203.7 jit_solution(14835057548060095699)
XLA Ops:
  0.6 3.5 %copy.67 = f32[1,8,8192]{1,2,0:T(8,128)} copy(f32[1,8,8192]{2,1,0:T(8,128)} %param.3) | data formatting | bytes 524288 | tf_op args[0]
  4.6 38.4 %reduce.8 = f32[8192,8]{1,0:T(8,128)} reduce(f32[8192,1,1,8]{3,2,1,0:T(1,128)} %bitcast.172, f32[]{:T(128)} %broadcast.468), dimensions={1,2}, to_apply=%bitcast.166.reduce_sub_computation | reduce | bytes 524292
  43.0 4.4 %reshape.683 = f32[16,1,4096]{2,1,0:T(1,128)} reshape(f32[8192,8]{1,0:T(8,128)} %reduce.8) | data formatting | bytes 524288
  47.4 12.9 %all-to-all-start = ((f32[16,1,4096]{2,1,0:T(1,128)}), f32[16,1,4096]{2,1,0:T(1,128)S(1)}, u32[]{:S(2)}, u32[]{:S(2)}) async-start(f32[16,1,4096]{2,1,0:T(1,128)} %reshape.683), calls=%async_computation | async-start | bytes 524288 | tf_op jit(solution)/shard_map/all_to_all | solution.py:117
  60.6 12.4 %all-to-all-done = f32[16,1,4096]{2,1,0:T(1,128)S(1)} async-done(((f32[16,1,4096]{2,1,0:T(1,128)}), f32[16,1,4096]{2,1,0:T(1,128)S(1)}, u32[]{:S(2)}, u32[]{:S(2)}) %all-to-all-start) | async-done | bytes 262176 | tf_op jit(solution)/shard_map/all_to_all | solution.py:117
  72.9 1.3 reduce.9
  74.2 8.4 %reshape.684 = f32[8192,1,1,8]{3,2,1,0:T(1,128)} reshape(f32[16,4096]{1,0:T(8,128)S(1)} %reduce.9) | data formatting | bytes 524288
  82.6 2.9 %copy.68 = f32[8,16,512]{2,1,0:T(8,128)S(1)} copy(f32[8,16,512]{0,2,1:T(8,128)} %bitcast.173) | data formatting | bytes 524288 | tf_op jit(solution)/shard_map/all_to_all | solution.py:117
  87.4 1.1 copy.74
  88.5 4.1 %all-to-all-start.1 = ((f32[1,8,2,16,512]{4,1,2,0,3:T(8,128)}), f32[1,8,2,16,512]{4,1,2,0,3:T(8,128)S(1)}, u32[]{:S(2)}, u32[]{:S(2)}) async-start(f32[1,8,2,16,512]{4,1,2,0,3:T(8,128)} %copy.74), calls=%async_computation.1 | async-start | bytes 1048576 | tf_op jit(solution)/shard_map/all_to_all | solution.py:126
  92.7 1.3 slice_reduce_fusion.3
  95.2 11.7 %all-to-all-done.1 = f32[1,8,2,16,512]{4,1,2,0,3:T(8,128)S(1)} async-done(((f32[1,8,2,16,512]{4,1,2,0,3:T(8,128)}), f32[1,8,2,16,512]{4,1,2,0,3:T(8,128)S(1)}, u32[]{:S(2)}, u32[]{:S(2)}) %all-to-all-start.1) | async-done | bytes 524320 | tf_op jit(solution)/shard_map/all_to_all | solution.py:126
  110.7 1.1 fusion.9
  117.7 1.2 fusion.5
  122.4 17.3 %all_to_all.45 = f32[16,1,4,2,1,512]{5,2,3,4,1,0:T(4,128)S(1)} all-to-all(f32[16,1,4,2,1,512]{5,2,3,4,1,0:T(4,128)S(1)} %get-tuple-element.17), channel_id=1, replica_groups=mesh['dp'=32,'ctx'=16] {'ctx'}, dimensions={0} | all-to-all | bytes 524288 | tf_op jit(solution)/shard_map/all_to_all | solution.py:34
  139.7 5.9 %all-to-all-start.2 = ((f32[16,1,4,2,1,512]{5,2,3,4,1,0:T(4,128)}), f32[16,1,4,2,1,512]{5,2,3,4,1,0:T(4,128)S(1)}, u32[]{:S(2)}, u32[]{:S(2)}) async-start(f32[16,1,4,2,1,512]{5,2,3,4,1,0:T(4,128)} %get-tuple-element.16), calls=%async_computation.2 | async-start | bytes 524288 | tf_op jit(solution)/shard_map/all_to_all | solution.py:34
  145.6 1.3 slice_reduce_fusion.1
  147.4 1.1 copy.92
  148.5 8.4 %all-to-all-done.2 = f32[16,1,4,2,1,512]{5,2,3,4,1,0:T(4,128)S(1)} async-done(((f32[16,1,4,2,1,512]{5,2,3,4,1,0:T(4,128)}), f32[16,1,4,2,1,512]{5,2,3,4,1,0:T(4,128)S(1)}, u32[]{:S(2)}, u32[]{:S(2)}) %all-to-all-start.2) | async-done | bytes 262176 | tf_op jit(solution)/shard_map/all_to_all | solution.py:34
  156.9 7.7 %all-to-all-start.5 = ((f32[32,8,2,256]{3,1,2,0:T(8,128)}), f32[32,8,2,256]{3,1,2,0:T(8,128)S(1)}, u32[]{:S(2)}, u32[]{:S(2)}) async-start(f32[32,8,2,256]{3,1,2,0:T(8,128)} %copy.92), calls=%async_computation.5 | async-start | bytes 1048576 | tf_op jit(solution)/shard_map/all_to_all | solution.py:40
  166.7 1.1 copy.90
  167.8 14.5 %all-to-all-done.5 = f32[32,8,2,256]{3,1,2,0:T(8,128)S(1)} async-done(((f32[32,8,2,256]{3,1,2,0:T(8,128)}), f32[32,8,2,256]{3,1,2,0:T(8,128)S(1)}, u32[]{:S(2)}, u32[]{:S(2)}) %all-to-all-start.5) | async-done | bytes 524320 | tf_op jit(solution)/shard_map/all_to_all | solution.py:40
  182.3 3.9 %all-to-all-start.4 = ((f32[1,8,2,16,512]{4,1,2,0,3:T(8,128)}), f32[1,8,2,16,512]{4,1,2,0,3:T(8,128)S(1)}, u32[]{:S(2)}, u32[]{:S(2)}) async-start(f32[1,8,2,16,512]{4,1,2,0,3:T(8,128)} %copy.90), calls=%async_computation.4 | async-start | bytes 1048576 | tf_op jit(solution)/shard_map/all_to_all | solution.py:139
  187.0 15.9 %all-to-all-done.4 = f32[1,8,2,16,512]{4,1,2,0,3:T(8,128)S(1)} async-done(((f32[1,8,2,16,512]{4,1,2,0,3:T(8,128)}), f32[1,8,2,16,512]{4,1,2,0,3:T(8,128)S(1)}, u32[]{:S(2)}, u32[]{:S(2)}) %all-to-all-start.4) | async-done | bytes 524320 | tf_op jit(solution)/shard_map/all_to_all | solution.py:139
  (63 shorter events, 20.8 us)
Async XLA Ops:
  47.4 25.5 %all-to-all-start = ((f32[16,1,4096]{2,1,0:T(1,128)}), f32[16,1,4096]{2,1,0:T(1,128)S(1)}, u32[]{:S(2)}, u32[]{:S(2)}) async-start(f32[16,1,4096]{2,1,0:T(1,128)} %reshape.683), calls=%async_computation | async-start | bytes 524288 | tf_op jit(solution)/shard_map/all_to_all | solution.py:117
  82.6 10.1 %copy-start = (f32[8,2,8192]{2,1,0:T(2,128)S(1)}, f32[8,2,8192]{2,1,0:T(2,128)}, u32[]{:S(2)}) copy-start(f32[8,2,8192]{2,1,0:T(2,128)} %param.5) | copy-start | bytes 1572868
  88.5 18.3 %all-to-all-start.1 = ((f32[1,8,2,16,512]{4,1,2,0,3:T(8,128)}), f32[1,8,2,16,512]{4,1,2,0,3:T(8,128)S(1)}, u32[]{:S(2)}, u32[]{:S(2)}) async-start(f32[1,8,2,16,512]{4,1,2,0,3:T(8,128)} %copy.74), calls=%async_computation.1 | async-start | bytes 1048576 | tf_op jit(solution)/shard_map/all_to_all | solution.py:126
  119.5 26.2 %copy-start.1 = (f32[1,8,2,8192]{3,2,1,0:T(2,128)S(1)}, f32[1,8,2,8192]{3,2,1,0:T(2,128)}, u32[]{:S(2)}) copy-start(f32[1,8,2,8192]{3,2,1,0:T(2,128)} %param.4) | copy-start | bytes 1572868
  139.7 17.1 %all-to-all-start.2 = ((f32[16,1,4,2,1,512]{5,2,3,4,1,0:T(4,128)}), f32[16,1,4,2,1,512]{5,2,3,4,1,0:T(4,128)S(1)}, u32[]{:S(2)}, u32[]{:S(2)}) async-start(f32[16,1,4,2,1,512]{5,2,3,4,1,0:T(4,128)} %get-tuple-element.16), calls=%async_computation.2 | async-start | bytes 524288 | tf_op jit(solution)/shard_map/all_to_all | solution.py:34
  156.9 25.4 %all-to-all-start.5 = ((f32[32,8,2,256]{3,1,2,0:T(8,128)}), f32[32,8,2,256]{3,1,2,0:T(8,128)S(1)}, u32[]{:S(2)}, u32[]{:S(2)}) async-start(f32[32,8,2,256]{3,1,2,0:T(8,128)} %copy.92), calls=%async_computation.5 | async-start | bytes 1048576 | tf_op jit(solution)/shard_map/all_to_all | solution.py:40
  182.3 20.6 %all-to-all-start.4 = ((f32[1,8,2,16,512]{4,1,2,0,3:T(8,128)}), f32[1,8,2,16,512]{4,1,2,0,3:T(8,128)S(1)}, u32[]{:S(2)}, u32[]{:S(2)}) async-start(f32[1,8,2,16,512]{4,1,2,0,3:T(8,128)} %copy.90), calls=%async_computation.4 | async-start | bytes 1048576 | tf_op jit(solution)/shard_map/all_to_all | solution.py:139
where the time goes:
time: 204 us
  waiting for transfers between devices  62.9 us (31%)
  other arithmetic  42.4 us (21%)
  starting transfers between devices  34.5 us (17%)
  local copies, waits for them, and re-layouts  28.9 us (14%)
  blocking collectives  17.3 us (8%)
  matrix products  16.7 us (8%)
    unnamed x1, other arithmetic  38.4 us
    unnamed x9, local copies, waits for them, and re-layouts  17.4 us
    all_to_all x1, blocking collectives, cut_exchange(): lax.all_to_all(piece, axis, split_axis=0, concat_axis=0, tiled=True)  17.3 us
    all_to_all x1, waiting for transfers between devices, inverse_transpose(): back = lax.all_to_all(mixed, 'ctx', split_axis=3, concat_axis=4, tiled=True)  15.9 us
    all_to_all x1, waiting for transfers between devices, sent_and_summed(): parts = lax.all_to_all(split_up(array, dim, peers), axis, 0, 0, tiled=True)  14.5 us
    all_to_all x1, starting transfers between devices, forward_transpose(): lax.all_to_all(samples[:, :, None, :], 'ctx', split_axis=3, concat_axis=2...  12.9 us
    all_to_all x1, waiting for transfers between devices, forward_transpose(): lax.all_to_all(samples[:, :, None, :], 'ctx', split_axis=3, concat_axis=2...  12.4 us
    all_to_all x1, waiting for transfers between devices, forward_transpose(): back = lax.all_to_all(mixed, 'ctx', split_axis=3, concat_axis=4, tiled=True)  11.7 us
  transfers between devices with their start and end apart: 5, of which 5 were waited for; matrix products, arithmetic and copies ran while one was open for 5% of the time, Pallas kernels for 0%

commit v1 on v0

v1 whole, which is shorter than its diff:
```python
import functools
import math

import jax
import jax.numpy as jnp
import numpy as np
from jax import lax
from jax.experimental import pallas as pl
from jax.experimental.pallas import tpu as pltpu
from jax.sharding import PartitionSpec as P

INTERPRET = False
RANKS = 16
CHANS = 8
LANES = 128
ROWS = 64
TOKENS = ROWS * LANES
LENGTH = RANKS * TOKENS
SLICE = TOKENS // RANKS
TILES = SLICE // LANES

VMEM = pl.BlockSpec(memory_space=pltpu.VMEM)
SMEM = pl.BlockSpec(memory_space=pltpu.SMEM)


def reversed_digits(index, sections=4):
    return sum((index >> level & 1) << sections - 1 - level for level in range(sections))


def rotor(angle_over_circle):
    angle = 2.0 * math.pi * angle_over_circle
    return (math.cos(angle), math.sin(angle))


def times(value, factor):
    real, imag = value
    cosine, sine = factor
    return (real * cosine - imag * sine, real * sine + imag * cosine)


def plus(left, right):
    return (left[0] + right[0], left[1] + right[1])


def minus(left, right):
    return (left[0] - right[0], left[1] - right[1])


def quarter(value, sign):
    real, imag = value
    return (-imag, real) if sign > 0 else (imag, -real)


def dft4(values, sign):
    even_sum, even_diff = plus(values[0], values[2]), minus(values[0], values[2])
    odd_sum, odd_diff = plus(values[1], values[3]), minus(values[1], values[3])
    turned = quarter(odd_diff, sign)
    return [plus(even_sum, odd_sum), plus(even_diff, turned), minus(even_sum, odd_sum), minus(even_diff, turned)]


def dft8(values, sign):
    even = dft4(values[0::2], sign)
    odd = dft4(values[1::2], sign)
    half = math.sqrt(0.5)
    real, imag = odd[1]
    one = ((real - imag) * half, (real + imag) * half) if sign > 0 else ((real + imag) * half, (imag - real) * half)
    real, imag = odd[3]
    three = ((-real - imag) * half, (real - imag) * half) if sign > 0 else ((imag - real) * half, (-real - imag) * half)
    odd = [odd[0], one, quarter(odd[2], sign), three]
    return [plus(even[k], odd[k]) for k in range(4)] + [minus(even[k], odd[k]) for k in range(4)]


def spread_kernel(samples_ref, out_ref):
    for tile in range(TILES):
        lanes = slice(tile * LANES, (tile + 1) * LANES)
        first = []
        for low in range(4):
            turned = []
            for high in range(4):
                sample = samples_ref[4 * high + low, :, lanes]
                cosine, sine = rotor(-high / 16)
                turned.append((sample * cosine, sample * sine))
            turned[0] = (samples_ref[low, :, lanes], jnp.zeros((CHANS, LANES), jnp.float32))
            first.append(dft4(turned, -1))
        for residue in range(4):
            last = [first[0][residue]] + [
                times(first[low][residue], rotor(-(4 * residue + 1) * low / 64)) for low in range(1, 4)
            ]
            for high, (real, imag) in enumerate(dft4(last, -1)):
                owner = reversed_digits(4 * high + residue)
                out_ref[owner, 0, :, lanes] = real
                out_ref[owner, 1, :, lanes] = imag


def gather_kernel(parts_ref, out_ref):
    for tile in range(TILES):
        lanes = slice(tile * LANES, (tile + 1) * LANES)
        first = []
        for residue in range(4):
            owners = [reversed_digits(4 * high + residue) for high in range(4)]
            values = dft4([(parts_ref[o, 0, :, lanes], parts_ref[o, 1, :, lanes]) for o in owners], 1)
            first.append(
                [values[0]] + [times(values[low], rotor((4 * residue + 1) * low / 64)) for low in range(1, 4)]
            )
        for low in range(4):
            values = dft4([first[residue][low] for residue in range(4)], 1)
            for high in range(4):
                cosine, sine = rotor(high / 16)
                real, imag = values[high]
                out_ref[4 * high + low, :, lanes] = real if high == 0 else real * cosine - imag * sine


def product(rows, high_ref, low_ref):
    high = rows.astype(jnp.bfloat16)
    low = (rows - high.astype(jnp.float32)).astype(jnp.bfloat16)
    dot = functools.partial(jnp.dot, preferred_element_type=jnp.float32)
    return dot(high, high_ref[...]) + dot(low, high_ref[...]) + dot(high, low_ref[...])


def local_kernel(
    mixed_ref, filter_ref, scalars_ref, shift_ref, middle_ref, there_high, there_low, back_high, back_low,
    out_ref, spectrum_ref, work_ref, twiddle_ref,
):
    shift = (shift_ref[0:1, :], shift_ref[1:2, :])
    real, imag = times((middle_ref[0], middle_ref[1]), shift)
    twiddle_ref[0] = real
    twiddle_ref[1] = imag

    def scalar(index, sign):
        return (scalars_ref[index, 0], scalars_ref[index, 1] * sign)

    def row(index, sign):
        whole = (CHANS, LANES)
        real = jnp.broadcast_to(twiddle_ref[0, index : index + 1, :], whole)
        imag = jnp.broadcast_to(twiddle_ref[1, index : index + 1, :], whole)
        return (real, imag if sign > 0 else -imag)

    def source(index):
        lanes = slice(index % TILES * LANES, (index % TILES + 1) * LANES)
        return index // TILES, lanes

    for inner in range(8):
        values = []
        for outer in range(8):
            rank, lanes = source(8 * outer + inner)
            value = (mixed_ref[rank, 0, :, lanes], mixed_ref[rank, 1, :, lanes])
            values.append(times(value, scalar(outer, 1)) if outer else value)
        values = dft8(values, -1)
        for a in range(8):
            real, imag = times(values[a], scalar(8 + 8 * inner + a, 1)) if inner else values[a]
            work_ref[8 * inner + a, :, :LANES] = real
            work_ref[8 * inner + a, :, LANES:] = imag
    for a in range(8):
        values = dft8(
            [(work_ref[8 * inner + a, :, :LANES], work_ref[8 * inner + a, :, LANES:]) for inner in range(8)], -1
        )
        for b in range(8):
            real, imag = times(values[b], row(a + 8 * b, 1))
            work_ref[8 * b + a, :, :LANES] = real
            work_ref[8 * b + a, :, LANES:] = imag

    spectrum = product(work_ref[...].reshape(ROWS * CHANS, 2 * LANES), there_high, there_low)
    spectrum_ref[...] = spectrum.reshape(ROWS, CHANS, 2 * LANES)
    filters = filter_ref[...].reshape(ROWS * CHANS, 2 * LANES)
    real, imag = times(
        (spectrum[:, :LANES], spectrum[:, LANES:]), (filters[:, :LANES], -filters[:, LANES:])
    )
    back = product(jnp.concatenate([real, imag], axis=1), back_high, back_low)
    work_ref[...] = back.reshape(ROWS, CHANS, 2 * LANES)

    for a in range(8):
        values = []
        for b in range(8):
            value = (work_ref[8 * b + a, :, :LANES], work_ref[8 * b + a, :, LANES:])
            values.append(times(value, row(a + 8 * b, -1)))
        values = dft8(values, 1)
        for inner in range(8):
            real, imag = times(values[inner], scalar(8 + 8 * inner + a, -1)) if inner else values[inner]
            work_ref[8 * inner + a, :, :LANES] = real
            work_ref[8 * inner + a, :, LANES:] = imag
    for inner in range(8):
        values = dft8(
            [(work_ref[8 * inner + a, :, :LANES], work_ref[8 * inner + a, :, LANES:]) for a in range(8)], 1
        )
        for outer in range(8):
            real, imag = times(values[outer], scalar(outer, -1)) if outer else values[outer]
            rank, lanes = source(8 * outer + inner)
            out_ref[rank, 0, :, lanes] = real
            out_ref[rank, 1, :, lanes] = imag


def term_kernel(spectrum_ref, saved_ref, out_ref):
    owners, rows = out_ref.shape[0], out_ref.shape[1] // 2
    spectrum = spectrum_ref[...].reshape(ROWS * CHANS, 2 * LANES)
    saved = saved_ref[...].reshape(ROWS * CHANS, 2 * LANES)
    term = times((spectrum[:, :LANES], spectrum[:, LANES:]), (saved[:, :LANES], -saved[:, LANES:]))
    for part in range(2):
        turned = term[part].T
        for owner in range(owners):
            out_ref[owner, part * rows : (part + 1) * rows, :] = turned[owner * rows : (owner + 1) * rows, :]


def call(kernel, out_shapes, in_specs, scratch=()):
    outs = [jax.ShapeDtypeStruct(shape, jnp.float32) for shape in out_shapes]
    return pl.pallas_call(
        kernel,
        out_shape=outs if len(outs) > 1 else outs[0],
        in_specs=in_specs,
        out_specs=[VMEM] * len(outs) if len(outs) > 1 else VMEM,
        scratch_shapes=list(scratch),
        interpret=INTERPRET,
    )


def split_table(table):
    table = table.astype(np.float32)
    high = table.astype(jnp.bfloat16)
    low = (table - high.astype(np.float32)).astype(jnp.bfloat16)
    return high, low


def tables():
    lane = np.arange(LANES)
    angle = 2.0 * np.pi / LANES * (lane[:, None] * lane[None, :] % LANES)
    cosine, sine = np.cos(angle), np.sin(angle)
    there = np.block([[cosine, -sine], [sine, cosine]])
    back = np.block([[cosine, sine], [-sine, cosine]]) / LENGTH
    middle_angle = -2.0 * np.pi / TOKENS * (np.arange(ROWS)[:, None] * lane[None, :])
    middle = np.stack([np.cos(middle_angle), np.sin(middle_angle)]).astype(np.float32)
    scalars = np.zeros((RANKS, 72, 2), np.float32)
    shift = np.zeros((RANKS, 2, LANES), np.float32)
    series = np.arange(8)
    for rank in range(RANKS):
        step = 4 * reversed_digits(rank) + 1
        outer = -2.0 * np.pi * step * 8 * series / 4096
        inner = -2.0 * np.pi * (step * series[:, None] / 4096 + series[:, None] * series[None, :] / 64)
        angles = np.concatenate([outer, inner.reshape(-1)])
        scalars[rank] = np.stack([np.cos(angles), np.sin(angles)], axis=1)
        lanes = -2.0 * np.pi * step * lane / (4 * LENGTH)
        shift[rank] = np.stack([np.cos(lanes), np.sin(lanes)])
    return split_table(there), split_table(back), middle, scalars, shift


def by_frequency(spectrum):
    parts = spectrum.reshape(CHANS, 2, LANES, ROWS)
    return jnp.transpose(parts, (3, 0, 1, 2)).reshape(ROWS, CHANS, 2 * LANES)


def per_device(output_gradient, input_spectrum, filter_spectrum):
    owners = lax.axis_size("dp")
    rank = lax.axis_index("ctx")
    there, back, middle, scalars, shift = tables()
    own = lambda table: lax.dynamic_index_in_dim(jnp.asarray(table), rank, 0, keepdims=False)
    exchange = lambda array, axis: lax.all_to_all(array, axis, split_axis=0, concat_axis=0, tiled=True)

    slices = jnp.transpose(output_gradient.reshape(CHANS, RANKS, SLICE), (1, 0, 2))
    samples = exchange(slices, "ctx")
    filters = by_frequency(filter_spectrum)
    saved = by_frequency(input_spectrum[0])
    mixed = call(spread_kernel, [(RANKS, 2, CHANS, SLICE)], [VMEM])(samples)
    mixed = exchange(mixed, "ctx")
    work = (ROWS, CHANS, 2 * LANES)
    parts, spectrum = call(
        local_kernel,
        [(RANKS, 2, CHANS, SLICE), work],
        [VMEM, VMEM, SMEM] + [VMEM] * 6,
        [pltpu.VMEM(work, jnp.float32), pltpu.VMEM((2, ROWS, LANES), jnp.float32)],
    )(mixed, filters, own(scalars), own(shift), middle, *there, *back)
    parts = exchange(parts, "ctx")
    term = call(term_kernel, [(owners, 2 * LANES // owners, ROWS * CHANS)], [VMEM, VMEM])(spectrum, saved)
    blocks = call(gather_kernel, [(RANKS, CHANS, SLICE)], [VMEM])(parts)
    blocks = exchange(blocks, "ctx")
    input_gradient = jnp.transpose(blocks, (1, 0, 2)).reshape(1, CHANS, TOKENS)

    total = jnp.sum(exchange(term, "dp"), axis=0)
    total = total.reshape(2, LANES // owners, ROWS, CHANS)
    filter_gradient = jnp.transpose(total, (3, 0, 1, 2)).reshape(CHANS, 2, TOKENS // owners)
    return (input_gradient, filter_gradient)


def solution(mesh):
    in_specs = (P("dp", None, "ctx"), P("dp", None, None, "ctx"), P(None, None, "ctx"))
    out_specs = (P("dp", None, "ctx"), P(None, None, ("ctx", "dp")))
    return jax.shard_map(
        per_device, mesh=mesh, in_specs=in_specs, out_specs=out_specs, check_vma=False
    )
```

time: 204 us -> 119 us (0.58)
  other arithmetic: 42.4 us -> 0.05 us
  local copies, waits for them, and re-layouts: 28.9 us -> 9.58 us
  matrix products: 16.7 us -> 0 us
  waiting for transfers between devices: 62.9 us -> 47.1 us
  Pallas kernels: 0 us -> 9.71 us
  starting transfers between devices: 34.5 us -> 25.2 us
  blocking collectives: 17.3 us -> 25.6 us
    unnamed x1 -> x0, other arithmetic: 38.4 us -> none
    dot_general x24 -> x0, matrix products: 16.7 us -> none  [the longest x6 4.35 us: complex_product(): jnp.einsum(form, left_imag, right_imag, precision=precise)]
    all_to_all x5 -> x4, waiting for transfers between devices: 62.9 us -> 47.1 us  [per_device(): lax.all_to_all(array, axis, split_axis=0, concat_axis=0, tiled=True)]
    unnamed x9 -> x12, local copies, waits for them, and re-layouts: 17.4 us -> 3.63 us
    pallas_call x0 -> x4, Pallas kernels: none -> 9.71 us  [the longest x1 3.68 us: per_device(): call(local_kernel, [(RANKS, 2, CHANS, SLICE), work], [VMEM, VMEM, SMEM] +...]
    all_to_all x5 -> x4, starting transfers between devices: 34.5 us -> 25.2 us  [per_device(): lax.all_to_all(array, axis, split_axis=0, concat_axis=0, tiled=True)]
    all_to_all x1, blocking collectives: 17.3 us -> 25.6 us  [per_device(): lax.all_to_all(array, axis, split_axis=0, concat_axis=0, tiled=True)]
    all_to_all x3 -> x0, local copies, waits for them, and re-layouts: 3.2 us -> none  [the longest x1 2.88 us: forward_transpose(): lax.all_to_all(samples[:, :, None, :], 'ctx', split_axis=3, concat_axis=2...]
  transfers between devices with their start and end apart: 5 -> 4, of which waited for: 5 -> 4; matrix products, arithmetic and copies ran while one was open for 5% -> 6% of each run, Pallas kernels for 0% -> 4%
where the time goes in v1:
time: 119 us; the launch traced here: 118 us
  waiting for transfers between devices  47.1 us (40%)
  blocking collectives  25.6 us (22%)
  starting transfers between devices  25.2 us (21%)
  Pallas kernels  9.71 us (8%)
  local copies, waits for them, and re-layouts  9.58 us (8%)
    all_to_all x4, waiting for transfers between devices, per_device(): lax.all_to_all(array, axis, split_axis=0, concat_axis=0, tiled=True)  47.1 us
    all_to_all x1, blocking collectives, per_device(): lax.all_to_all(array, axis, split_axis=0, concat_axis=0, tiled=True)  25.6 us
    all_to_all x4, starting transfers between devices, per_device(): lax.all_to_all(array, axis, split_axis=0, concat_axis=0, tiled=True)  25.2 us
    pallas_call x1, Pallas kernels, per_device(): call(local_kernel, [(RANKS, 2, CHANS, SLICE), work], [VMEM, VMEM, SMEM] +...  3.68 us
    unnamed x12, local copies, waits for them, and re-layouts  3.63 us
    squeeze x2, local copies, waits for them, and re-layouts, per_device(): lax.dynamic_index_in_dim(jnp.asarray(table), rank, 0, keepdims=False)  2.63 us
  transfers between devices with their start and end apart: 4, of which 4 were waited for; matrix products, arithmetic and copies ran while one was open for 6% of the time, Pallas kernels for 4%

profile of v1, /device:TPU:8, one launch (start us, length us, event | category | flops | bytes accessed | tf_op | source)
XLA Modules:
  0.0 118.0 jit_solution(1118541074917873724)
XLA Ops:
  0.6 25.6 %all_to_all.25.samples_ref = f32[16,8,512]{2,1,0:T(8,128)} all-to-all(f32[16,8,512]{2,1,0:T(8,128)} %bitcast.29), channel_id=1, replica_groups=mesh['dp'=32,'ctx'=16] {'ctx'}, dimensions={0} | all-to-all | bytes 524288 | tf_op jit(solution)/shard_map/all_to_all | solution.py:254
  26.2 1.9 %shard_map.113 = f32[16,2,8,512]{3,2,1,0:T(8,128)} custom-call(f32[16,8,512]{2,1,0:T(8,128)} %all_to_all.25.samples_ref), custom_call_target="tpu_custom_call" | custom-call | tf_op jit(solution)/shard_map/pallas_call | solution.py:260
  28.1 4.1 %all-to-all-start.1 = ((f32[16,2,8,512]{3,2,1,0:T(8,128)}), f32[16,2,8,512]{3,2,1,0:T(8,128)S(1)}, u32[]{:S(2)}, u32[]{:S(2)}) async-start(f32[16,2,8,512]{3,2,1,0:T(8,128)} %shard_map.113), calls=%async_computation.1 | async-start | bytes 1048576 | tf_op jit(solution)/shard_map/all_to_all | solution.py:254
  32.2 0.3 copy.14
  32.5 0.4 reshape.26
  32.9 1.2 %copy.15 = f32[64,8,2,128]{3,1,2,0:T(8,128)} copy(f32[64,8,2,128]{0,3,1,2:T(8,128)S(1)} %bitcast.23) | data formatting | bytes 1048576 | tf_op jit(solution)/shard_map/transpose | solution.py:246
  34.1 1.2 %dynamic-slice_bitcast_fusion.1.shift_ref = f32[2,128]{1,0:T(2,128)} fusion(f32[16,2,128]{2,1,0:T(2,128)} %constant.31.clone, s32[]{:T(128)S(6)} %select_n.6), kind=kLoop, calls=%fused_computation.1 | loop fusion | bytes 2052 | tf_op jit(solution)/shard_map/jit(dynamic_index_in_dim)/squeeze | solution.py:253
  35.4 1.4 %dynamic-slice_bitcast_fusion.scalars_ref = f32[72,2]{1,0:T(8,128)} fusion(f32[16,72,2]{2,1,0:T(8,128)} %constant.30.clone, s32[]{:T(128)S(6)} %select_n.6), kind=kLoop, calls=%fused_computation | loop fusion | bytes 1156 | tf_op jit(solution)/shard_map/jit(dynamic_index_in_dim)/squeeze | solution.py:253
  36.8 9.8 %all-to-all-done.1.mixed_ref = f32[16,2,8,512]{3,2,1,0:T(8,128)S(1)} async-done(((f32[16,2,8,512]{3,2,1,0:T(8,128)}), f32[16,2,8,512]{3,2,1,0:T(8,128)S(1)}, u32[]{:S(2)}, u32[]{:S(2)}) %all-to-all-start.1) | async-done | bytes 524320 | tf_op jit(solution)/shard_map/all_to_all | solution.py:254
  46.6 0.8 copy-done
  47.4 3.7 %shard_map.114 = (f32[16,2,8,512]{3,2,1,0:T(8,128)}, f32[64,8,256]{2,1,0:T(8,128)}) custom-call(f32[16,2,8,512]{3,2,1,0:T(8,128)} %copy-done, f32[64,8,256]{2,1,0:T(8,128)} %bitcast.25, f32[72,2]{1,0:T(8,128)} %dynamic-slice_bitcast_fusion.scalars_ref, f32[2,128]{1,0:T(2,128)} %dynamic-slice_bitcast_fusion.1.shift_ref, ...), custom_call_target="tpu_custom_call" | custom-call | tf_op jit(solution)/shard_map/pallas_call | solution.py:263
  51.1 6.4 %all-to-all-start.2 = ((f32[16,2,8,512]{3,2,1,0:T(8,128)}), f32[16,2,8,512]{3,2,1,0:T(8,128)S(1)}, u32[]{:S(2)}, u32[]{:S(2)}) async-start(f32[16,2,8,512]{3,2,1,0:T(8,128)} %get-tuple-element.4), calls=%async_computation.2 | async-start | bytes 1048576 | tf_op jit(solution)/shard_map/all_to_all | solution.py:254
  57.8 0.4 reshape_squeeze.3
  58.2 1.2 copy.17
  59.4 2.3 %shard_map.116 = f32[32,8,512]{2,1,0:T(8,128)} custom-call(f32[64,8,256]{2,1,0:T(8,128)} %get-tuple-element.5.spectrum_ref, f32[64,8,256]{2,1,0:T(8,128)} %bitcast.26), custom_call_target="tpu_custom_call" | custom-call | tf_op jit(solution)/shard_map/pallas_call | solution.py:270
  61.7 10.9 %all-to-all-done.2.parts_ref = f32[16,2,8,512]{3,2,1,0:T(8,128)S(1)} async-done(((f32[16,2,8,512]{3,2,1,0:T(8,128)}), f32[16,2,8,512]{3,2,1,0:T(8,128)S(1)}, u32[]{:S(2)}, u32[]{:S(2)}) %all-to-all-start.2) | async-done | bytes 524320 | tf_op jit(solution)/shard_map/all_to_all | solution.py:254
  72.6 0.8 copy-done.1
  73.4 8.9 %all-to-all-start.4 = ((f32[32,8,512]{2,1,0:T(8,128)}), f32[32,8,512]{2,1,0:T(8,128)S(1)}, u32[]{:S(2)}, u32[]{:S(2)}) async-start(f32[32,8,512]{2,1,0:T(8,128)} %shard_map.116), calls=%async_computation.4 | async-start | bytes 1048576 | tf_op jit(solution)/shard_map/all_to_all | solution.py:254
  82.3 1.9 %shard_map.115 = f32[16,8,512]{2,1,0:T(8,128)} custom-call(f32[16,2,8,512]{3,2,1,0:T(8,128)} %copy-done.1), custom_call_target="tpu_custom_call" | custom-call | tf_op jit(solution)/shard_map/pallas_call | solution.py:271
  84.2 15.8 %all-to-all-done.4 = f32[32,8,512]{2,1,0:T(8,128)S(1)} async-done(((f32[32,8,512]{2,1,0:T(8,128)}), f32[32,8,512]{2,1,0:T(8,128)S(1)}, u32[]{:S(2)}, u32[]{:S(2)}) %all-to-all-start.4) | async-done | bytes 524320 | tf_op jit(solution)/shard_map/all_to_all | solution.py:254
  100.0 5.8 %all-to-all-start.3 = ((f32[16,8,512]{2,1,0:T(8,128)}), f32[16,8,512]{2,1,0:T(8,128)S(1)}, u32[]{:S(2)}, u32[]{:S(2)}) async-start(f32[16,8,512]{2,1,0:T(8,128)} %shard_map.115), calls=%async_computation.3 | async-start | bytes 524288 | tf_op jit(solution)/shard_map/all_to_all | solution.py:254
  106.0 0.7 copy.18
  106.7 10.5 %all-to-all-done.3 = f32[16,8,512]{2,1,0:T(8,128)S(1)} async-done(((f32[16,8,512]{2,1,0:T(8,128)}), f32[16,8,512]{2,1,0:T(8,128)S(1)}, u32[]{:S(2)}, u32[]{:S(2)}) %all-to-all-start.3) | async-done | bytes 262176 | tf_op jit(solution)/shard_map/all_to_all | solution.py:254
  117.3 0.7 copy.20
  (9 shorter events, 0.5 us)
Async XLA Ops:
  28.1 4.1 %copy-start.2 = (f32[8,2,8192]{2,1,0:T(2,128)S(1)}, f32[8,2,8192]{2,1,0:T(2,128)}, u32[]{:S(2)}) copy-start(f32[8,2,8192]{2,1,0:T(2,128)} %param.12) | copy-start | bytes 1572868
  28.1 18.5 %all-to-all-start.1 = ((f32[16,2,8,512]{3,2,1,0:T(8,128)}), f32[16,2,8,512]{3,2,1,0:T(8,128)S(1)}, u32[]{:S(2)}, u32[]{:S(2)}) async-start(f32[16,2,8,512]{3,2,1,0:T(8,128)} %shard_map.113), calls=%async_computation.1 | async-start | bytes 1048576 | tf_op jit(solution)/shard_map/all_to_all | solution.py:254
  46.6 0.8 copy-start
  51.1 6.4 %copy-start.3 = (f32[1,8,2,8192]{3,2,1,0:T(2,128)S(1)}, f32[1,8,2,8192]{3,2,1,0:T(2,128)}, u32[]{:S(2)}) copy-start(f32[1,8,2,8192]{3,2,1,0:T(2,128)} %param.11) | copy-start | bytes 1572868
  51.1 21.5 %all-to-all-start.2 = ((f32[16,2,8,512]{3,2,1,0:T(8,128)}), f32[16,2,8,512]{3,2,1,0:T(8,128)S(1)}, u32[]{:S(2)}, u32[]{:S(2)}) async-start(f32[16,2,8,512]{3,2,1,0:T(8,128)} %get-tuple-element.4), calls=%async_computation.2 | async-start | bytes 1048576 | tf_op jit(solution)/shard_map/all_to_all | solution.py:254
  72.6 0.8 copy-start.1
  73.4 26.6 %all-to-all-start.4 = ((f32[32,8,512]{2,1,0:T(8,128)}), f32[32,8,512]{2,1,0:T(8,128)S(1)}, u32[]{:S(2)}, u32[]{:S(2)}) async-start(f32[32,8,512]{2,1,0:T(8,128)} %shard_map.116), calls=%async_computation.4 | async-start | bytes 1048576 | tf_op jit(solution)/shard_map/all_to_all | solution.py:254
  100.0 17.3 %all-to-all-start.3 = ((f32[16,8,512]{2,1,0:T(8,128)}), f32[16,8,512]{2,1,0:T(8,128)S(1)}, u32[]{:S(2)}, u32[]{:S(2)}) async-start(f32[16,8,512]{2,1,0:T(8,128)} %shard_map.115), calls=%async_computation.3 | async-start | bytes 524288 | tf_op jit(solution)/shard_map/all_to_all | solution.py:254

commit v2 on v1

--- a/solution.py
+++ b/solution.py
@@ -189,27 +189,54 @@
             out_ref[rank, 1, :, lanes] = imag
 
 
-def term_kernel(spectrum_ref, saved_ref, out_ref):
-    owners, rows = out_ref.shape[0], out_ref.shape[1] // 2
+def term_kernel(rank_ref, spectrum_ref, saved_ref, keep_ref, send_ref):
+    owners, rows = 2 * keep_ref.shape[0], keep_ref.shape[1] // 2
+    rank = rank_ref[0]
     spectrum = spectrum_ref[...].reshape(ROWS * CHANS, 2 * LANES)
     saved = saved_ref[...].reshape(ROWS * CHANS, 2 * LANES)
     term = times((spectrum[:, :LANES], spectrum[:, LANES:]), (saved[:, :LANES], -saved[:, LANES:]))
-    for part in range(2):
-        turned = term[part].T
-        for owner in range(owners):
-            out_ref[owner, part * rows : (part + 1) * rows, :] = turned[owner * rows : (owner + 1) * rows, :]
-
-
-def call(kernel, out_shapes, in_specs, scratch=()):
-    outs = [jax.ShapeDtypeStruct(shape, jnp.float32) for shape in out_shapes]
+    turned = [part.T for part in term]
+    for pair in range(owners // 2):
+        apart = rank >> 1 ^ pair
+        slot = (apart & 3) << 2 | apart >> 2
+        for part in range(2):
+            place = slice(part * rows, (part + 1) * rows)
+            even = turned[part][2 * pair * rows : (2 * pair + 1) * rows, :]
+            odd = turned[part][(2 * pair + 1) * rows : (2 * pair + 2) * rows, :]
+            keep_ref[slot, place, :] = jnp.where(rank & 1 == 0, even, odd)
+            send_ref[slot, place, :] = jnp.where(rank & 1 == 0, odd, even)
+
+
+def summed(total, sent):
+    for array in sent:
+        total = total + array
+    return total
+
+
+def sum_over_sequences(keep, send, owners):
+    def swap(array, apart):
+        return lax.ppermute(array, "dp", [(i, i ^ apart) for i in range(owners)])
+
+    total = keep + swap(send, 1)
+    total = total.reshape(4, 4, *keep.shape[1:])
+    total = summed(total[0], [swap(total[k], k << 1) for k in range(1, 4)])
+    return summed(total[0], [swap(total[k], k << 3) for k in range(1, 4)])
+
+
+def call(kernel, outs, in_specs, scratch=()):
+    specs = [pl.BlockSpec(memory_space=out.memory_space) for out in outs]
     return pl.pallas_call(
         kernel,
         out_shape=outs if len(outs) > 1 else outs[0],
         in_specs=in_specs,
-        out_specs=[VMEM] * len(outs) if len(outs) > 1 else VMEM,
+        out_specs=specs if len(specs) > 1 else specs[0],
         scratch_shapes=list(scratch),
         interpret=INTERPRET,
     )
+
+
+def on_chip(array):
+    return array if INTERPRET else pltpu.with_memory_space_constraint(array, pltpu.VMEM)
 
 
 def split_table(table):
@@ -257,22 +284,24 @@
     samples = exchange(slices, "ctx")
     filters = by_frequency(filter_spectrum)
     saved = by_frequency(input_spectrum[0])
-    mixed = call(spread_kernel, [(RANKS, 2, CHANS, SLICE)], [VMEM])(samples)
+    mixed = call(spread_kernel, [pltpu.VMEM((RANKS, 2, CHANS, SLICE), jnp.float32)], [VMEM])(on_chip(samples))
     mixed = exchange(mixed, "ctx")
     work = (ROWS, CHANS, 2 * LANES)
     parts, spectrum = call(
         local_kernel,
-        [(RANKS, 2, CHANS, SLICE), work],
+        [pltpu.VMEM((RANKS, 2, CHANS, SLICE), jnp.float32), pltpu.VMEM(work, jnp.float32)],
         [VMEM, VMEM, SMEM] + [VMEM] * 6,
         [pltpu.VMEM(work, jnp.float32), pltpu.VMEM((2, ROWS, LANES), jnp.float32)],
-    )(mixed, filters, own(scalars), own(shift), middle, *there, *back)
+    )(on_chip(mixed), on_chip(filters), own(scalars), own(shift), middle, *there, *back)
     parts = exchange(parts, "ctx")
-    term = call(term_kernel, [(owners, 2 * LANES // owners, ROWS * CHANS)], [VMEM, VMEM])(spectrum, saved)
-    blocks = call(gather_kernel, [(RANKS, CHANS, SLICE)], [VMEM])(parts)
+    half = pltpu.VMEM((owners // 2, 2 * LANES // owners, ROWS * CHANS), jnp.float32)
+    keep, send = call(term_kernel, [half, half], [SMEM, VMEM, VMEM])(
+        lax.axis_index("dp").reshape(1), on_chip(spectrum), on_chip(saved)
+    )
+    total = sum_over_sequences(keep, send, owners)
+    blocks = call(gather_kernel, [pltpu.VMEM((RANKS, CHANS, SLICE), jnp.float32)], [VMEM])(on_chip(parts))
     blocks = exchange(blocks, "ctx")
     input_gradient = jnp.transpose(blocks, (1, 0, 2)).reshape(1, CHANS, TOKENS)
-
-    total = jnp.sum(exchange(term, "dp"), axis=0)
     total = total.reshape(2, LANES // owners, ROWS, CHANS)
     filter_gradient = jnp.transpose(total, (3, 0, 1, 2)).reshape(CHANS, 2, TOKENS // owners)
     return (input_gradient, filter_gradient)

time: 119 us -> 105 us (0.88)
  the two profiles are of different devices: /device:TPU:8 before, /device:TPU:2 now
where the time goes in v2:
time: 105 us; the launch traced here: 104 us
  starting transfers between devices  48.7 us (46%)
  blocking collectives  24.3 us (23%)
  waiting for transfers between devices  17.9 us (17%)
  local copies, waits for them, and re-layouts  6.46 us (6%)
  Pallas kernels  5.67 us (5%)
    ppermute x7, starting transfers between devices, swap(): return lax.ppermute(array, 'dp', [(i, i ^ apart) for i in range(owners)])  25.2 us
    all_to_all x1, blocking collectives, per_device(): lax.all_to_all(array, axis, split_axis=0, concat_axis=0, tiled=True)  24.3 us
    all_to_all x3, starting transfers between devices, per_device(): lax.all_to_all(array, axis, split_axis=0, concat_axis=0, tiled=True)  23.5 us
    all_to_all x3, waiting for transfers between devices, per_device(): lax.all_to_all(array, axis, split_axis=0, concat_axis=0, tiled=True)  8.95 us
    ppermute x7, waiting for transfers between devices, swap(): return lax.ppermute(array, 'dp', [(i, i ^ apart) for i in range(owners)])  8.93 us
    pallas_call x1, Pallas kernels, per_device(): call(local_kernel, [pltpu.VMEM((RANKS, 2, CHANS, SLICE), jnp.float32), pl...  3.62 us
    squeeze x2, local copies, waits for them, and re-layouts, per_device(): lax.dynamic_index_in_dim(jnp.asarray(table), rank, 0, keepdims=False)  2.63 us
  transfers between devices with their start and end apart: 10, of which 4 were waited for; matrix products, arithmetic and copies ran while one was open for 6% of the time, Pallas kernels for 1%

profile of v2, /device:TPU:2, one launch (start us, length us, event | category | flops | bytes accessed | tf_op | source)
XLA Modules:
  0.0 103.9 jit_solution(11790274905219136708)
XLA Ops:
  0.6 24.3 %all_to_all.20.samples_ref = f32[16,8,512]{2,1,0:T(8,128)S(1)} all-to-all(f32[16,8,512]{2,1,0:T(8,128)} %bitcast.44), channel_id=1, replica_groups=mesh['dp'=32,'ctx'=16] {'ctx'}, dimensions={0} | all-to-all | bytes 524288 | tf_op jit(solution)/shard_map/all_to_all | solution.py:281
  24.9 0.9 shard_map.113
  25.8 5.8 %all-to-all-start.1 = ((f32[16,2,8,512]{3,2,1,0:T(8,128)}), f32[16,2,8,512]{3,2,1,0:T(8,128)S(1)}, u32[]{:S(2)}, u32[]{:S(2)}) async-start(f32[16,2,8,512]{3,2,1,0:T(8,128)} %shard_map.113), calls=%async_computation.1 | async-start | bytes 1048576 | tf_op jit(solution)/shard_map/all_to_all | solution.py:281
  31.9 0.4 reshape.38
  32.7 1.2 %dynamic-slice_bitcast_fusion.1.shift_ref = f32[2,128]{1,0:T(2,128)} fusion(f32[16,2,128]{2,1,0:T(2,128)} %constant.34.clone, s32[]{:T(128)S(6)} %select_n.6), kind=kLoop, calls=%fused_computation.11 | loop fusion | bytes 2052 | tf_op jit(solution)/shard_map/jit(dynamic_index_in_dim)/squeeze | solution.py:280
  34.0 1.4 %dynamic-slice_bitcast_fusion.scalars_ref = f32[72,2]{1,0:T(8,128)} fusion(f32[16,72,2]{2,1,0:T(8,128)} %constant.33.clone, s32[]{:T(128)S(6)} %select_n.6), kind=kLoop, calls=%fused_computation.3 | loop fusion | bytes 1156 | tf_op jit(solution)/shard_map/jit(dynamic_index_in_dim)/squeeze | solution.py:280
  35.4 8.9 %all-to-all-done.1.mixed_ref = f32[16,2,8,512]{3,2,1,0:T(8,128)S(1)} async-done(((f32[16,2,8,512]{3,2,1,0:T(8,128)}), f32[16,2,8,512]{3,2,1,0:T(8,128)S(1)}, u32[]{:S(2)}, u32[]{:S(2)}) %all-to-all-start.1) | async-done | bytes 524320 | tf_op jit(solution)/shard_map/all_to_all | solution.py:281
  44.3 3.6 %shard_map.114 = (f32[16,2,8,512]{3,2,1,0:T(8,128)}, f32[64,8,256]{2,1,0:T(8,128)S(1)}) custom-call(f32[16,2,8,512]{3,2,1,0:T(8,128)S(1)} %all-to-all-done.1.mixed_ref, f32[64,8,256]{2,1,0:T(8,128)S(1)} %bitcast.38, f32[72,2]{1,0:T(8,128)} %dynamic-slice_bitcast_fusion.scalars_ref, f32[2,128]{1,0:T(2,128)} %dynamic-slice_bitcast_fusion.1.shift_ref, ...), custom_call_target="tpu_custom_call" | custom-call | tf_op jit(solution)/shard_map/pallas_call | solution.py:290
  47.9 8.1 %all-to-all-start.2 = ((f32[16,2,8,512]{3,2,1,0:T(8,128)}), f32[16,2,8,512]{3,2,1,0:T(8,128)S(1)}, u32[]{:S(2)}, u32[]{:S(2)}) async-start(f32[16,2,8,512]{3,2,1,0:T(8,128)} %get-tuple-element.6), calls=%async_computation.2 | async-start | bytes 1048576 | tf_op jit(solution)/shard_map/all_to_all | solution.py:281
  56.4 0.4 reshape_squeeze.3
  57.4 1.9 %collective-permute-start = (f32[16,8,512]{2,1,0:T(8,128)S(1)}, f32[16,8,512]{2,1,0:T(8,128)S(1)}, u32[]{:S(2)}, u32[]{:S(2)}) collective-permute-start(f32[16,8,512]{2,1,0:T(8,128)S(1)} %get-tuple-element.9), channel_id=1, source_target_pairs={{0,16},{16,0},{32,48},{48,32},{64,80},{80,64},{96,112},{112,96},{1... | collective-permute-start | bytes 786440 | tf_op jit(solution)/shard_map/ppermute | solution.py:218
  59.4 1.5 %collective-permute-done = f32[16,8,512]{2,1,0:T(8,128)S(1)} collective-permute-done((f32[16,8,512]{2,1,0:T(8,128)S(1)}, f32[16,8,512]{2,1,0:T(8,128)S(1)}, u32[]{:S(2)}, u32[]{:S(2)}) %collective-permute-start) | collective-permute-done | bytes 262176 | tf_op jit(solution)/shard_map/ppermute | solution.py:218
  60.9 5.5 %collective-permute-start.3 = (f32[4,8,512]{2,1,0:T(8,128)S(1)}, f32[4,8,512]{2,1,0:T(8,128)S(1)}, u32[]{:S(2)}, u32[]{:S(2)}) collective-permute-start(f32[4,8,512]{2,1,0:T(8,128)S(1)} %get-tuple-element.13), channel_id=1, source_target_pairs={{0,96},{16,112},{32,64},{48,80},{64,32},{80,48},{96,0},{112,16},{1... | collective-permute-start | bytes 196616 | tf_op jit(solution)/shard_map/ppermute | solution.py:218
  66.5 1.9 %collective-permute-start.2 = (f32[4,8,512]{2,1,0:T(8,128)S(1)}, f32[4,8,512]{2,1,0:T(8,128)S(1)}, u32[]{:S(2)}, u32[]{:S(2)}) collective-permute-start(f32[4,8,512]{2,1,0:T(8,128)S(1)} %get-tuple-element.14), channel_id=1, source_target_pairs={{0,64},{16,80},{32,96},{48,112},{64,0},{80,16},{96,32},{112,48},{1... | collective-permute-start | bytes 196616 | tf_op jit(solution)/shard_map/ppermute | solution.py:218
  68.4 2.7 %collective-permute-start.1 = (f32[4,8,512]{2,1,0:T(8,128)S(1)}, f32[4,8,512]{2,1,0:T(8,128)S(1)}, u32[]{:S(2)}, u32[]{:S(2)}) collective-permute-start(f32[4,8,512]{2,1,0:T(8,128)S(1)} %get-tuple-element.12), channel_id=1, source_target_pairs={{0,32},{16,48},{32,0},{48,16},{64,96},{80,112},{96,64},{112,80},{1... | collective-permute-start | bytes 196616 | tf_op jit(solution)/shard_map/ppermute | solution.py:218
  71.1 0.8 shard_map.115
  71.9 9.6 %all-to-all-start.3 = ((f32[16,8,512]{2,1,0:T(8,128)}), f32[16,8,512]{2,1,0:T(8,128)S(1)}, u32[]{:S(2)}, u32[]{:S(2)}) async-start(f32[16,8,512]{2,1,0:T(8,128)} %shard_map.115), calls=%async_computation.3 | async-start | bytes 524288 | tf_op jit(solution)/shard_map/all_to_all | solution.py:281
  81.6 8.8 %collective-permute-start.6 = (f32[8,512]{1,0:T(8,128)S(1)}, f32[8,512]{1,0:T(8,128)S(1)}, u32[]{:S(2)}, u32[]{:S(2)}) collective-permute-start(f32[8,512]{1,0:T(8,128)S(1)} %get-tuple-element.16), channel_id=1, source_target_pairs={{0,384},{16,400},{32,416},{48,432},{64,448},{80,464},{96,480},{112... | collective-permute-start | bytes 49160 | tf_op jit(solution)/shard_map/ppermute | solution.py:218
  90.4 2.3 %collective-permute-start.5 = (f32[8,512]{1,0:T(8,128)S(1)}, f32[8,512]{1,0:T(8,128)S(1)}, u32[]{:S(2)}, u32[]{:S(2)}) collective-permute-start(f32[8,512]{1,0:T(8,128)S(1)} %get-tuple-element.17), channel_id=1, source_target_pairs={{0,256},{16,272},{32,288},{48,304},{64,320},{80,336},{96,352},{112... | collective-permute-start | bytes 49160 | tf_op jit(solution)/shard_map/ppermute | solution.py:218
  92.7 2.1 %collective-permute-start.4 = (f32[8,512]{1,0:T(8,128)S(1)}, f32[8,512]{1,0:T(8,128)S(1)}, u32[]{:S(2)}, u32[]{:S(2)}) collective-permute-start(f32[8,512]{1,0:T(8,128)S(1)} %get-tuple-element.15), channel_id=1, source_target_pairs={{0,128},{16,144},{32,160},{48,176},{64,192},{80,208},{96,224},{112... | collective-permute-start | bytes 49160 | tf_op jit(solution)/shard_map/ppermute | solution.py:218
  94.9 1.2 %collective-permute-done.5 = f32[8,512]{1,0:T(8,128)S(1)} collective-permute-done((f32[8,512]{1,0:T(8,128)S(1)}, f32[8,512]{1,0:T(8,128)S(1)}, u32[]{:S(2)}, u32[]{:S(2)}) %collective-permute-start.5) | collective-permute-done | bytes 16416 | tf_op jit(solution)/shard_map/ppermute | solution.py:218
  96.1 6.2 %collective-permute-done.4 = f32[8,512]{1,0:T(8,128)S(1)} collective-permute-done((f32[8,512]{1,0:T(8,128)S(1)}, f32[8,512]{1,0:T(8,128)S(1)}, u32[]{:S(2)}, u32[]{:S(2)}) %collective-permute-start.4) | collective-permute-done | bytes 16416 | tf_op jit(solution)/shard_map/ppermute | solution.py:218
  102.5 0.7 copy.19
  103.2 0.7 copy.21
  (21 shorter events, 1.9 us)
Async XLA Ops:
  25.8 5.8 %copy-start = (f32[8,2,8192]{2,1,0:T(2,128)S(1)}, f32[8,2,8192]{2,1,0:T(2,128)}, u32[]{:S(2)}) copy-start(f32[8,2,8192]{2,1,0:T(2,128)} %param.12) | copy-start | bytes 1572868
  25.8 18.5 %all-to-all-start.1 = ((f32[16,2,8,512]{3,2,1,0:T(8,128)}), f32[16,2,8,512]{3,2,1,0:T(8,128)S(1)}, u32[]{:S(2)}, u32[]{:S(2)}) async-start(f32[16,2,8,512]{3,2,1,0:T(8,128)} %shard_map.113), calls=%async_computation.1 | async-start | bytes 1048576 | tf_op jit(solution)/shard_map/all_to_all | solution.py:281
  47.9 8.1 %copy-start.1 = (f32[1,8,2,8192]{3,2,1,0:T(2,128)S(1)}, f32[1,8,2,8192]{3,2,1,0:T(2,128)}, u32[]{:S(2)}) copy-start(f32[1,8,2,8192]{3,2,1,0:T(2,128)} %param.11) | copy-start | bytes 1572868
  47.9 23.1 %all-to-all-start.2 = ((f32[16,2,8,512]{3,2,1,0:T(8,128)}), f32[16,2,8,512]{3,2,1,0:T(8,128)S(1)}, u32[]{:S(2)}, u32[]{:S(2)}) async-start(f32[16,2,8,512]{3,2,1,0:T(8,128)} %get-tuple-element.6), calls=%async_computation.2 | async-start | bytes 1048576 | tf_op jit(solution)/shard_map/all_to_all | solution.py:281
  57.4 3.4 %collective-permute-start = (f32[16,8,512]{2,1,0:T(8,128)S(1)}, f32[16,8,512]{2,1,0:T(8,128)S(1)}, u32[]{:S(2)}, u32[]{:S(2)}) collective-permute-start(f32[16,8,512]{2,1,0:T(8,128)S(1)} %get-tuple-element.9), channel_id=1, source_target_pairs={{0,16},{16,0},{32,48},{48,32},{64,80},{80,64},{96,112},{112,96},{1... | collective-permute-start | bytes 786440 | tf_op jit(solution)/shard_map/ppermute | solution.py:218
  60.9 20.6 %collective-permute-start.3 = (f32[4,8,512]{2,1,0:T(8,128)S(1)}, f32[4,8,512]{2,1,0:T(8,128)S(1)}, u32[]{:S(2)}, u32[]{:S(2)}) collective-permute-start(f32[4,8,512]{2,1,0:T(8,128)S(1)} %get-tuple-element.13), channel_id=1, source_target_pairs={{0,96},{16,112},{32,64},{48,80},{64,32},{80,48},{96,0},{112,16},{1... | collective-permute-start | bytes 196616 | tf_op jit(solution)/shard_map/ppermute | solution.py:218
  66.5 15.1 %collective-permute-start.2 = (f32[4,8,512]{2,1,0:T(8,128)S(1)}, f32[4,8,512]{2,1,0:T(8,128)S(1)}, u32[]{:S(2)}, u32[]{:S(2)}) collective-permute-start(f32[4,8,512]{2,1,0:T(8,128)S(1)} %get-tuple-element.14), channel_id=1, source_target_pairs={{0,64},{16,80},{32,96},{48,112},{64,0},{80,16},{96,32},{112,48},{1... | collective-permute-start | bytes 196616 | tf_op jit(solution)/shard_map/ppermute | solution.py:218
  68.4 13.2 %collective-permute-start.1 = (f32[4,8,512]{2,1,0:T(8,128)S(1)}, f32[4,8,512]{2,1,0:T(8,128)S(1)}, u32[]{:S(2)}, u32[]{:S(2)}) collective-permute-start(f32[4,8,512]{2,1,0:T(8,128)S(1)} %get-tuple-element.12), channel_id=1, source_target_pairs={{0,32},{16,48},{32,0},{48,16},{64,96},{80,112},{96,64},{112,80},{1... | collective-permute-start | bytes 196616 | tf_op jit(solution)/shard_map/ppermute | solution.py:218
  71.9 31.2 %all-to-all-start.3 = ((f32[16,8,512]{2,1,0:T(8,128)}), f32[16,8,512]{2,1,0:T(8,128)S(1)}, u32[]{:S(2)}, u32[]{:S(2)}) async-start(f32[16,8,512]{2,1,0:T(8,128)} %shard_map.115), calls=%async_computation.3 | async-start | bytes 524288 | tf_op jit(solution)/shard_map/all_to_all | solution.py:281
  81.6 13.2 %collective-permute-start.6 = (f32[8,512]{1,0:T(8,128)S(1)}, f32[8,512]{1,0:T(8,128)S(1)}, u32[]{:S(2)}, u32[]{:S(2)}) collective-permute-start(f32[8,512]{1,0:T(8,128)S(1)} %get-tuple-element.16), channel_id=1, source_target_pairs={{0,384},{16,400},{32,416},{48,432},{64,448},{80,464},{96,480},{112... | collective-permute-start | bytes 49160 | tf_op jit(solution)/shard_map/ppermute | solution.py:218
  90.4 5.6 %collective-permute-start.5 = (f32[8,512]{1,0:T(8,128)S(1)}, f32[8,512]{1,0:T(8,128)S(1)}, u32[]{:S(2)}, u32[]{:S(2)}) collective-permute-start(f32[8,512]{1,0:T(8,128)S(1)} %get-tuple-element.17), channel_id=1, source_target_pairs={{0,256},{16,272},{32,288},{48,304},{64,320},{80,336},{96,352},{112... | collective-permute-start | bytes 49160 | tf_op jit(solution)/shard_map/ppermute | solution.py:218
  92.7 9.5 %collective-permute-start.4 = (f32[8,512]{1,0:T(8,128)S(1)}, f32[8,512]{1,0:T(8,128)S(1)}, u32[]{:S(2)}, u32[]{:S(2)}) collective-permute-start(f32[8,512]{1,0:T(8,128)S(1)} %get-tuple-element.15), channel_id=1, source_target_pairs={{0,128},{16,144},{32,160},{48,176},{64,192},{80,208},{96,224},{112... | collective-permute-start | bytes 49160 | tf_op jit(solution)/shard_map/ppermute | solution.py:218

commit v3 on v2

--- a/solution.py
+++ b/solution.py
@@ -117,73 +117,81 @@
     return dot(high, high_ref[...]) + dot(low, high_ref[...]) + dot(high, low_ref[...])
 
 
-def local_kernel(
-    mixed_ref, filter_ref, scalars_ref, shift_ref, middle_ref, there_high, there_low, back_high, back_low,
-    out_ref, spectrum_ref, work_ref, twiddle_ref,
+def twiddles(shift_ref, middle_ref, twiddle_ref):
+    shift = (shift_ref[0:1, :], shift_ref[1:2, :])
+    twiddle_ref[0], twiddle_ref[1] = times((middle_ref[0], middle_ref[1]), shift)
+
+
+def twiddle_row(twiddle_ref, index, sign):
+    whole = (CHANS, LANES)
+    real = jnp.broadcast_to(twiddle_ref[0, index : index + 1, :], whole)
+    imag = jnp.broadcast_to(twiddle_ref[1, index : index + 1, :], whole)
+    return (real, imag if sign > 0 else -imag)
+
+
+def source(index):
+    lanes = slice(index % TILES * LANES, (index % TILES + 1) * LANES)
+    return index // TILES, lanes
+
+
+def load(ref, index):
+    return (ref[index, :, :LANES], ref[index, :, LANES:])
+
+
+def store(ref, index, value):
+    ref[index, :, :LANES], ref[index, :, LANES:] = value
+
+
+def forward_kernel(
+    mixed_ref, scalars_ref, shift_ref, middle_ref, high_ref, low_ref, spectrum_ref, work_ref, twiddle_ref
 ):
-    shift = (shift_ref[0:1, :], shift_ref[1:2, :])
-    real, imag = times((middle_ref[0], middle_ref[1]), shift)
-    twiddle_ref[0] = real
-    twiddle_ref[1] = imag
-
-    def scalar(index, sign):
-        return (scalars_ref[index, 0], scalars_ref[index, 1] * sign)
-
-    def row(index, sign):
-        whole = (CHANS, LANES)
-        real = jnp.broadcast_to(twiddle_ref[0, index : index + 1, :], whole)
-        imag = jnp.broadcast_to(twiddle_ref[1, index : index + 1, :], whole)
-        return (real, imag if sign > 0 else -imag)
-
-    def source(index):
-        lanes = slice(index % TILES * LANES, (index % TILES + 1) * LANES)
-        return index // TILES, lanes
+    twiddles(shift_ref, middle_ref, twiddle_ref)
+
+    def scalar(index):
+        return twiddle_row(scalars_ref, index, 1)
 
     for inner in range(8):
         values = []
         for outer in range(8):
             rank, lanes = source(8 * outer + inner)
             value = (mixed_ref[rank, 0, :, lanes], mixed_ref[rank, 1, :, lanes])
-            values.append(times(value, scalar(outer, 1)) if outer else value)
+            values.append(times(value, scalar(outer)) if outer else value)
         values = dft8(values, -1)
         for a in range(8):
-            real, imag = times(values[a], scalar(8 + 8 * inner + a, 1)) if inner else values[a]
-            work_ref[8 * inner + a, :, :LANES] = real
-            work_ref[8 * inner + a, :, LANES:] = imag
+            store(work_ref, 8 * inner + a, times(values[a], scalar(8 + 8 * inner + a)) if inner else values[a])
     for a in range(8):
-        values = dft8(
-            [(work_ref[8 * inner + a, :, :LANES], work_ref[8 * inner + a, :, LANES:]) for inner in range(8)], -1
-        )
+        values = dft8([load(work_ref, 8 * inner + a) for inner in range(8)], -1)
         for b in range(8):
-            real, imag = times(values[b], row(a + 8 * b, 1))
-            work_ref[8 * b + a, :, :LANES] = real
-            work_ref[8 * b + a, :, LANES:] = imag
-
-    spectrum = product(work_ref[...].reshape(ROWS * CHANS, 2 * LANES), there_high, there_low)
+            store(work_ref, 8 * b + a, times(values[b], twiddle_row(twiddle_ref, a + 8 * b, 1)))
+    spectrum = product(work_ref[...].reshape(ROWS * CHANS, 2 * LANES), high_ref, low_ref)
     spectrum_ref[...] = spectrum.reshape(ROWS, CHANS, 2 * LANES)
+
+
+def inverse_kernel(
+    spectrum_ref, filter_ref, scalars_ref, shift_ref, middle_ref, high_ref, low_ref, out_ref, work_ref, twiddle_ref
+):
+    twiddles(shift_ref, middle_ref, twiddle_ref)
+
+    def scalar(index):
+        return twiddle_row(scalars_ref, index, -1)
+
+    spectrum = spectrum_ref[...].reshape(ROWS * CHANS, 2 * LANES)
     filters = filter_ref[...].reshape(ROWS * CHANS, 2 * LANES)
-    real, imag = times(
-        (spectrum[:, :LANES], spectrum[:, LANES:]), (filters[:, :LANES], -filters[:, LANES:])
-    )
-    back = product(jnp.concatenate([real, imag], axis=1), back_high, back_low)
+    real, imag = times((spectrum[:, :LANES], spectrum[:, LANES:]), (filters[:, :LANES], -filters[:, LANES:]))
+    back = product(jnp.concatenate([real, imag], axis=1), high_ref, low_ref)
     work_ref[...] = back.reshape(ROWS, CHANS, 2 * LANES)
-
     for a in range(8):
         values = []
         for b in range(8):
-            value = (work_ref[8 * b + a, :, :LANES], work_ref[8 * b + a, :, LANES:])
-            values.append(times(value, row(a + 8 * b, -1)))
+            values.append(times(load(work_ref, 8 * b + a), twiddle_row(twiddle_ref, a + 8 * b, -1)))
         values = dft8(values, 1)
         for inner in range(8):
-            real, imag = times(values[inner], scalar(8 + 8 * inner + a, -1)) if inner else values[inner]
-            work_ref[8 * inner + a, :, :LANES] = real
-            work_ref[8 * inner + a, :, LANES:] = imag
+            value = values[inner]
+            store(work_ref, 8 * inner + a, times(value, scalar(8 + 8 * inner + a)) if inner else value)
     for inner in range(8):
-        values = dft8(
-            [(work_ref[8 * inner + a, :, :LANES], work_ref[8 * inner + a, :, LANES:]) for a in range(8)], 1
-        )
+        values = dft8([load(work_ref, 8 * inner + a) for a in range(8)], 1)
         for outer in range(8):
-            real, imag = times(values[outer], scalar(outer, -1)) if outer else values[outer]
+            real, imag = times(values[outer], scalar(outer)) if outer else values[outer]
             rank, lanes = source(8 * outer + inner)
             out_ref[rank, 0, :, lanes] = real
             out_ref[rank, 1, :, lanes] = imag
@@ -287,18 +295,26 @@
     mixed = call(spread_kernel, [pltpu.VMEM((RANKS, 2, CHANS, SLICE), jnp.float32)], [VMEM])(on_chip(samples))
     mixed = exchange(mixed, "ctx")
     work = (ROWS, CHANS, 2 * LANES)
-    parts, spectrum = call(
-        local_kernel,
-        [pltpu.VMEM((RANKS, 2, CHANS, SLICE), jnp.float32), pltpu.VMEM(work, jnp.float32)],
-        [VMEM, VMEM, SMEM] + [VMEM] * 6,
-        [pltpu.VMEM(work, jnp.float32), pltpu.VMEM((2, ROWS, LANES), jnp.float32)],
-    )(on_chip(mixed), on_chip(filters), own(scalars), own(shift), middle, *there, *back)
-    parts = exchange(parts, "ctx")
+    scratch = [pltpu.VMEM(work, jnp.float32), pltpu.VMEM((2, ROWS, LANES), jnp.float32)]
+    scalars = on_chip(jnp.broadcast_to(own(scalars).T[:, :, None], (2, 72, LANES)))
+    shift = on_chip(own(shift))
+    middle = on_chip(jnp.asarray(middle))
+    there, back = ([on_chip(jnp.asarray(table)) for table in pair] for pair in (there, back))
+    spectrum = call(
+        forward_kernel, [pltpu.VMEM(work, jnp.float32)], [VMEM] * 6, scratch
+    )(on_chip(mixed), scalars, shift, middle, *there)
     half = pltpu.VMEM((owners // 2, 2 * LANES // owners, ROWS * CHANS), jnp.float32)
     keep, send = call(term_kernel, [half, half], [SMEM, VMEM, VMEM])(
         lax.axis_index("dp").reshape(1), on_chip(spectrum), on_chip(saved)
     )
     total = sum_over_sequences(keep, send, owners)
+    parts = call(
+        inverse_kernel,
+        [pltpu.VMEM((RANKS, 2, CHANS, SLICE), jnp.float32)],
+        [VMEM] * 7,
+        scratch,
+    )(on_chip(spectrum), on_chip(filters), scalars, shift, middle, *back)
+    parts = exchange(parts, "ctx")
     blocks = call(gather_kernel, [pltpu.VMEM((RANKS, CHANS, SLICE), jnp.float32)], [VMEM])(on_chip(parts))
     blocks = exchange(blocks, "ctx")
     input_gradient = jnp.transpose(blocks, (1, 0, 2)).reshape(1, CHANS, TOKENS)

time: 105 us -> 100 us (0.952)
  the two profiles are of different devices: /device:TPU:2 before, /device:TPU:10 now
where the time goes in v3:
time: 100 us; the launch traced here: 99.4 us
  starting transfers between devices  48.6 us (49%)
  blocking collectives  24.3 us (24%)
  waiting for transfers between devices  15.8 us (16%)
  local copies, waits for them, and re-layouts  5.65 us (6%)
  Pallas kernels  4.13 us (4%)
    ppermute x7, starting transfers between devices, swap(): return lax.ppermute(array, 'dp', [(i, i ^ apart) for i in range(owners)])  25.2 us
    all_to_all x1, blocking collectives, per_device(): lax.all_to_all(array, axis, split_axis=0, concat_axis=0, tiled=True)  24.3 us
    all_to_all x3, starting transfers between devices, per_device(): lax.all_to_all(array, axis, split_axis=0, concat_axis=0, tiled=True)  23.5 us
    all_to_all x3, waiting for transfers between devices, per_device(): lax.all_to_all(array, axis, split_axis=0, concat_axis=0, tiled=True)  10.2 us
    ppermute x7, waiting for transfers between devices, swap(): return lax.ppermute(array, 'dp', [(i, i ^ apart) for i in range(owners)])  5.64 us
    unnamed x18, local copies, waits for them, and re-layouts  2.41 us
  transfers between devices with their start and end apart: 10, of which 3 were waited for; matrix products, arithmetic and copies ran while one was open for 5% of the time, Pallas kernels for 1%

profile of v3, /device:TPU:10, one launch (start us, length us, event | category | flops | bytes accessed | tf_op | source)
XLA Modules:
  0.0 99.4 jit_solution(11158253106071059162)
XLA Ops:
  0.6 24.3 %all_to_all.20.samples_ref = f32[16,8,512]{2,1,0:T(8,128)S(1)} all-to-all(f32[16,8,512]{2,1,0:T(8,128)} %bitcast.46), channel_id=1, replica_groups=mesh['dp'=32,'ctx'=16] {'ctx'}, dimensions={0} | all-to-all | bytes 524288 | tf_op jit(solution)/shard_map/all_to_all | solution.py:289
  24.9 0.9 shard_map.113
  25.8 5.8 %all-to-all-start.1 = ((f32[16,2,8,512]{3,2,1,0:T(8,128)}), f32[16,2,8,512]{3,2,1,0:T(8,128)S(1)}, u32[]{:S(2)}, u32[]{:S(2)}) async-start(f32[16,2,8,512]{3,2,1,0:T(8,128)} %shard_map.113), calls=%async_computation.1 | async-start | bytes 1048576 | tf_op jit(solution)/shard_map/all_to_all | solution.py:289
  31.9 0.4 reshape.39
  32.8 0.7 dynamic-slice_bitcast_fusion.shift_ref
  33.5 0.7 dynamic-slice_bitcast_fusion.1
  34.2 10.2 %all-to-all-done.1.mixed_ref = f32[16,2,8,512]{3,2,1,0:T(8,128)S(1)} async-done(((f32[16,2,8,512]{3,2,1,0:T(8,128)}), f32[16,2,8,512]{3,2,1,0:T(8,128)S(1)}, u32[]{:S(2)}, u32[]{:S(2)}) %all-to-all-start.1) | async-done | bytes 524320 | tf_op jit(solution)/shard_map/all_to_all | solution.py:289
  44.4 0.6 shard_map.114.spectrum_ref
  45.4 1.5 %shard_map.115 = f32[16,2,8,512]{3,2,1,0:T(8,128)} custom-call(f32[64,8,256]{2,1,0:T(8,128)S(1)} %shard_map.114.spectrum_ref, f32[64,8,256]{2,1,0:T(8,128)S(1)} %bitcast.40, f32[2,72,128]{2,1,0:T(8,128)S(1)} %broadcast_in_dim.2.scalars_ref, f32[2,128]{1,0:T(2,128)S(1)} %dynamic-slice_bitcast_fusion.shift_ref, f32[2,64,128]{2,1,0:T(8,128)S(1)} %copy-done, ...), custom_call_target="tpu_custom_call" | custom-call | tf_op jit(solution)/shard_map/pallas_call | solution.py:311
  46.8 8.1 %all-to-all-start.2 = ((f32[16,2,8,512]{3,2,1,0:T(8,128)}), f32[16,2,8,512]{3,2,1,0:T(8,128)S(1)}, u32[]{:S(2)}, u32[]{:S(2)}) async-start(f32[16,2,8,512]{3,2,1,0:T(8,128)} %shard_map.115), calls=%async_computation.2 | async-start | bytes 1048576 | tf_op jit(solution)/shard_map/all_to_all | solution.py:289
  55.3 0.4 reshape_squeeze.3
  56.4 1.9 %collective-permute-start = (f32[16,8,512]{2,1,0:T(8,128)S(1)}, f32[16,8,512]{2,1,0:T(8,128)S(1)}, u32[]{:S(2)}, u32[]{:S(2)}) collective-permute-start(f32[16,8,512]{2,1,0:T(8,128)S(1)} %get-tuple-element.5), channel_id=1, source_target_pairs={{0,16},{16,0},{32,48},{48,32},{64,80},{80,64},{96,112},{112,96},{1... | collective-permute-start | bytes 786440 | tf_op jit(solution)/shard_map/ppermute | solution.py:226
  58.3 1.5 %collective-permute-done = f32[16,8,512]{2,1,0:T(8,128)S(1)} collective-permute-done((f32[16,8,512]{2,1,0:T(8,128)S(1)}, f32[16,8,512]{2,1,0:T(8,128)S(1)}, u32[]{:S(2)}, u32[]{:S(2)}) %collective-permute-start) | collective-permute-done | bytes 262176 | tf_op jit(solution)/shard_map/ppermute | solution.py:226
  59.9 2.4 %collective-permute-start.1 = (f32[4,8,512]{2,1,0:T(8,128)S(1)}, f32[4,8,512]{2,1,0:T(8,128)S(1)}, u32[]{:S(2)}, u32[]{:S(2)}) collective-permute-start(f32[4,8,512]{2,1,0:T(8,128)S(1)} %get-tuple-element.8), channel_id=1, source_target_pairs={{0,32},{16,48},{32,0},{48,16},{64,96},{80,112},{96,64},{112,80},{1... | collective-permute-start | bytes 196616 | tf_op jit(solution)/shard_map/ppermute | solution.py:226
  62.2 4.6 %collective-permute-start.3 = (f32[4,8,512]{2,1,0:T(8,128)S(1)}, f32[4,8,512]{2,1,0:T(8,128)S(1)}, u32[]{:S(2)}, u32[]{:S(2)}) collective-permute-start(f32[4,8,512]{2,1,0:T(8,128)S(1)} %get-tuple-element.9), channel_id=1, source_target_pairs={{0,96},{16,112},{32,64},{48,80},{64,32},{80,48},{96,0},{112,16},{1... | collective-permute-start | bytes 196616 | tf_op jit(solution)/shard_map/ppermute | solution.py:226
  66.8 3.2 %collective-permute-start.2 = (f32[4,8,512]{2,1,0:T(8,128)S(1)}, f32[4,8,512]{2,1,0:T(8,128)S(1)}, u32[]{:S(2)}, u32[]{:S(2)}) collective-permute-start(f32[4,8,512]{2,1,0:T(8,128)S(1)} %get-tuple-element.10), channel_id=1, source_target_pairs={{0,64},{16,80},{32,96},{48,112},{64,0},{80,16},{96,32},{112,48},{1... | collective-permute-start | bytes 196616 | tf_op jit(solution)/shard_map/ppermute | solution.py:226
  70.0 0.8 shard_map.116
  70.9 9.6 %all-to-all-start.3 = ((f32[16,8,512]{2,1,0:T(8,128)}), f32[16,8,512]{2,1,0:T(8,128)S(1)}, u32[]{:S(2)}, u32[]{:S(2)}) async-start(f32[16,8,512]{2,1,0:T(8,128)} %shard_map.116), calls=%async_computation.3 | async-start | bytes 524288 | tf_op jit(solution)/shard_map/all_to_all | solution.py:289
  80.6 6.8 %collective-permute-start.4 = (f32[8,512]{1,0:T(8,128)S(1)}, f32[8,512]{1,0:T(8,128)S(1)}, u32[]{:S(2)}, u32[]{:S(2)}) collective-permute-start(f32[8,512]{1,0:T(8,128)S(1)} %get-tuple-element.11), channel_id=1, source_target_pairs={{0,128},{16,144},{32,160},{48,176},{64,192},{80,208},{96,224},{112... | collective-permute-start | bytes 49160 | tf_op jit(solution)/shard_map/ppermute | solution.py:226
  87.4 4.0 %collective-permute-start.6 = (f32[8,512]{1,0:T(8,128)S(1)}, f32[8,512]{1,0:T(8,128)S(1)}, u32[]{:S(2)}, u32[]{:S(2)}) collective-permute-start(f32[8,512]{1,0:T(8,128)S(1)} %get-tuple-element.12), channel_id=1, source_target_pairs={{0,384},{16,400},{32,416},{48,432},{64,448},{80,464},{96,480},{112... | collective-permute-start | bytes 49160 | tf_op jit(solution)/shard_map/ppermute | solution.py:226
  91.4 2.3 %collective-permute-start.5 = (f32[8,512]{1,0:T(8,128)S(1)}, f32[8,512]{1,0:T(8,128)S(1)}, u32[]{:S(2)}, u32[]{:S(2)}) collective-permute-start(f32[8,512]{1,0:T(8,128)S(1)} %get-tuple-element.13), channel_id=1, source_target_pairs={{0,256},{16,272},{32,288},{48,304},{64,320},{80,336},{96,352},{112... | collective-permute-start | bytes 49160 | tf_op jit(solution)/shard_map/ppermute | solution.py:226
  93.7 4.1 %collective-permute-done.6 = f32[8,512]{1,0:T(8,128)S(1)} collective-permute-done((f32[8,512]{1,0:T(8,128)S(1)}, f32[8,512]{1,0:T(8,128)S(1)}, u32[]{:S(2)}, u32[]{:S(2)}) %collective-permute-start.6) | collective-permute-done | bytes 16416 | tf_op jit(solution)/shard_map/ppermute | solution.py:226
  98.0 0.7 copy.19
  98.7 0.7 copy.21
  (33 shorter events, 2.4 us)
Async XLA Ops:
  25.8 5.8 %copy-start.5 = (f32[8,2,8192]{2,1,0:T(2,128)S(1)}, f32[8,2,8192]{2,1,0:T(2,128)}, u32[]{:S(2)}) copy-start(f32[8,2,8192]{2,1,0:T(2,128)} %param.12) | copy-start | bytes 1572868
  25.8 18.5 %all-to-all-start.1 = ((f32[16,2,8,512]{3,2,1,0:T(8,128)}), f32[16,2,8,512]{3,2,1,0:T(8,128)S(1)}, u32[]{:S(2)}, u32[]{:S(2)}) async-start(f32[16,2,8,512]{3,2,1,0:T(8,128)} %shard_map.113), calls=%async_computation.1 | async-start | bytes 1048576 | tf_op jit(solution)/shard_map/all_to_all | solution.py:289
  32.3 12.1 %copy-start.3 = (bf16[256,256]{1,0:T(8,128)(2,1)S(1)}, bf16[256,256]{1,0:T(8,128)(2,1)}, u32[]{:S(2)}) copy-start(bf16[256,256]{1,0:T(8,128)(2,1)} %constant.37.clone.low_ref) | copy-start | bytes 393220
  32.3 12.1 %copy-start.4 = (bf16[256,256]{1,0:T(8,128)(2,1)S(1)}, bf16[256,256]{1,0:T(8,128)(2,1)}, u32[]{:S(2)}) copy-start(bf16[256,256]{1,0:T(8,128)(2,1)} %constant.36.clone.high_ref) | copy-start | bytes 393220
  32.7 11.7 %copy-start = (f32[2,64,128]{2,1,0:T(8,128)S(1)}, f32[2,64,128]{2,1,0:T(8,128)}, u32[]{:S(2)}) copy-start(f32[2,64,128]{2,1,0:T(8,128)} %constant.35.clone.middle_ref) | copy-start | bytes 196612
  44.4 0.9 copy-start.1
  44.4 1.0 copy-start.2
  46.8 8.1 %copy-start.6 = (f32[1,8,2,8192]{3,2,1,0:T(2,128)S(1)}, f32[1,8,2,8192]{3,2,1,0:T(2,128)}, u32[]{:S(2)}) copy-start(f32[1,8,2,8192]{3,2,1,0:T(2,128)} %param.11) | copy-start | bytes 1572868
  46.8 23.2 %all-to-all-start.2 = ((f32[16,2,8,512]{3,2,1,0:T(8,128)}), f32[16,2,8,512]{3,2,1,0:T(8,128)S(1)}, u32[]{:S(2)}, u32[]{:S(2)}) async-start(f32[16,2,8,512]{3,2,1,0:T(8,128)} %shard_map.115), calls=%async_computation.2 | async-start | bytes 1048576 | tf_op jit(solution)/shard_map/all_to_all | solution.py:289
  56.4 3.4 %collective-permute-start = (f32[16,8,512]{2,1,0:T(8,128)S(1)}, f32[16,8,512]{2,1,0:T(8,128)S(1)}, u32[]{:S(2)}, u32[]{:S(2)}) collective-permute-start(f32[16,8,512]{2,1,0:T(8,128)S(1)} %get-tuple-element.5), channel_id=1, source_target_pairs={{0,16},{16,0},{32,48},{48,32},{64,80},{80,64},{96,112},{112,96},{1... | collective-permute-start | bytes 786440 | tf_op jit(solution)/shard_map/ppermute | solution.py:226
  59.9 20.6 %collective-permute-start.1 = (f32[4,8,512]{2,1,0:T(8,128)S(1)}, f32[4,8,512]{2,1,0:T(8,128)S(1)}, u32[]{:S(2)}, u32[]{:S(2)}) collective-permute-start(f32[4,8,512]{2,1,0:T(8,128)S(1)} %get-tuple-element.8), channel_id=1, source_target_pairs={{0,32},{16,48},{32,0},{48,16},{64,96},{80,112},{96,64},{112,80},{1... | collective-permute-start | bytes 196616 | tf_op jit(solution)/shard_map/ppermute | solution.py:226
  62.2 18.3 %collective-permute-start.3 = (f32[4,8,512]{2,1,0:T(8,128)S(1)}, f32[4,8,512]{2,1,0:T(8,128)S(1)}, u32[]{:S(2)}, u32[]{:S(2)}) collective-permute-start(f32[4,8,512]{2,1,0:T(8,128)S(1)} %get-tuple-element.9), channel_id=1, source_target_pairs={{0,96},{16,112},{32,64},{48,80},{64,32},{80,48},{96,0},{112,16},{1... | collective-permute-start | bytes 196616 | tf_op jit(solution)/shard_map/ppermute | solution.py:226
  66.8 13.7 %collective-permute-start.2 = (f32[4,8,512]{2,1,0:T(8,128)S(1)}, f32[4,8,512]{2,1,0:T(8,128)S(1)}, u32[]{:S(2)}, u32[]{:S(2)}) collective-permute-start(f32[4,8,512]{2,1,0:T(8,128)S(1)} %get-tuple-element.10), channel_id=1, source_target_pairs={{0,64},{16,80},{32,96},{48,112},{64,0},{80,16},{96,32},{112,48},{1... | collective-permute-start | bytes 196616 | tf_op jit(solution)/shard_map/ppermute | solution.py:226
  70.9 27.9 %all-to-all-start.3 = ((f32[16,8,512]{2,1,0:T(8,128)}), f32[16,8,512]{2,1,0:T(8,128)S(1)}, u32[]{:S(2)}, u32[]{:S(2)}) async-start(f32[16,8,512]{2,1,0:T(8,128)} %shard_map.116), calls=%async_computation.3 | async-start | bytes 524288 | tf_op jit(solution)/shard_map/all_to_all | solution.py:289
  80.6 13.1 %collective-permute-start.4 = (f32[8,512]{1,0:T(8,128)S(1)}, f32[8,512]{1,0:T(8,128)S(1)}, u32[]{:S(2)}, u32[]{:S(2)}) collective-permute-start(f32[8,512]{1,0:T(8,128)S(1)} %get-tuple-element.11), channel_id=1, source_target_pairs={{0,128},{16,144},{32,160},{48,176},{64,192},{80,208},{96,224},{112... | collective-permute-start | bytes 49160 | tf_op jit(solution)/shard_map/ppermute | solution.py:226
  87.4 10.4 %collective-permute-start.6 = (f32[8,512]{1,0:T(8,128)S(1)}, f32[8,512]{1,0:T(8,128)S(1)}, u32[]{:S(2)}, u32[]{:S(2)}) collective-permute-start(f32[8,512]{1,0:T(8,128)S(1)} %get-tuple-element.12), channel_id=1, source_target_pairs={{0,384},{16,400},{32,416},{48,432},{64,448},{80,464},{96,480},{112... | collective-permute-start | bytes 49160 | tf_op jit(solution)/shard_map/ppermute | solution.py:226
  91.4 6.4 %collective-permute-start.5 = (f32[8,512]{1,0:T(8,128)S(1)}, f32[8,512]{1,0:T(8,128)S(1)}, u32[]{:S(2)}, u32[]{:S(2)}) collective-permute-start(f32[8,512]{1,0:T(8,128)S(1)} %get-tuple-element.13), channel_id=1, source_target_pairs={{0,256},{16,272},{32,288},{48,304},{64,320},{80,336},{96,352},{112... | collective-permute-start | bytes 49160 | tf_op jit(solution)/shard_map/ppermute | solution.py:226

commit v4 on v3

--- a/solution.py
+++ b/solution.py
@@ -70,7 +70,8 @@
     return [plus(even[k], odd[k]) for k in range(4)] + [minus(even[k], odd[k]) for k in range(4)]
 
 
-def spread_kernel(samples_ref, out_ref):
+def spread_kernel(samples_ref, sent_ref, out_ref, semaphores):
+    copies = []
     for tile in range(TILES):
         lanes = slice(tile * LANES, (tile + 1) * LANES)
         first = []
@@ -90,9 +91,15 @@
                 owner = reversed_digits(4 * high + residue)
                 out_ref[owner, 0, :, lanes] = real
                 out_ref[owner, 1, :, lanes] = imag
-
-
-def gather_kernel(parts_ref, out_ref):
+        where = (slice(None), slice(None), slice(None), lanes)
+        copies.append(pltpu.make_async_copy(out_ref.at[where], sent_ref.at[where], semaphores.at[tile]))
+        copies[-1].start()
+    for copy in copies:
+        copy.wait()
+
+
+def gather_kernel(parts_ref, sent_ref, out_ref, semaphores):
+    copies = []
     for tile in range(TILES):
         lanes = slice(tile * LANES, (tile + 1) * LANES)
         first = []
@@ -108,6 +115,11 @@
                 cosine, sine = rotor(high / 16)
                 real, imag = values[high]
                 out_ref[4 * high + low, :, lanes] = real if high == 0 else real * cosine - imag * sine
+        where = (slice(None), slice(None), lanes)
+        copies.append(pltpu.make_async_copy(out_ref.at[where], sent_ref.at[where], semaphores.at[tile]))
+        copies[-1].start()
+    for copy in copies:
+        copy.wait()
 
 
 def product(rows, high_ref, low_ref):
@@ -206,7 +218,7 @@
     turned = [part.T for part in term]
     for pair in range(owners // 2):
         apart = rank >> 1 ^ pair
-        slot = (apart & 3) << 2 | apart >> 2
+        slot = (apart >> 1 & 3) << 2 | apart >> 3 << 1 | apart & 1
         for part in range(2):
             place = slice(part * rows, (part + 1) * rows)
             even = turned[part][2 * pair * rows : (2 * pair + 1) * rows, :]
@@ -227,8 +239,8 @@
 
     total = keep + swap(send, 1)
     total = total.reshape(4, 4, *keep.shape[1:])
-    total = summed(total[0], [swap(total[k], k << 1) for k in range(1, 4)])
-    return summed(total[0], [swap(total[k], k << 3) for k in range(1, 4)])
+    total = summed(total[0], [swap(total[k], (0, 4, 8, 12)[k]) for k in range(1, 4)])
+    return summed(total[0], [swap(total[k], (0, 2, 16, 18)[k]) for k in range(1, 4)])
 
 
 def call(kernel, outs, in_specs, scratch=()):
@@ -243,6 +255,10 @@
     )
 
 
+def leaving(shape, count):
+    return [pltpu.VMEM(shape, jnp.float32), pltpu.SemaphoreType.DMA((count,))]
+
+
 def on_chip(array):
     return array if INTERPRET else pltpu.with_memory_space_constraint(array, pltpu.VMEM)
 
@@ -259,7 +275,7 @@
     angle = 2.0 * np.pi / LANES * (lane[:, None] * lane[None, :] % LANES)
     cosine, sine = np.cos(angle), np.sin(angle)
     there = np.block([[cosine, -sine], [sine, cosine]])
-    back = np.block([[cosine, sine], [-sine, cosine]]) / LENGTH
+    back = np.block([[cosine, sine], [-sine, cosine]])
     middle_angle = -2.0 * np.pi / TOKENS * (np.arange(ROWS)[:, None] * lane[None, :])
     middle = np.stack([np.cos(middle_angle), np.sin(middle_angle)]).astype(np.float32)
     scalars = np.zeros((RANKS, 72, 2), np.float32)
@@ -288,11 +304,12 @@
     own = lambda table: lax.dynamic_index_in_dim(jnp.asarray(table), rank, 0, keepdims=False)
     exchange = lambda array, axis: lax.all_to_all(array, axis, split_axis=0, concat_axis=0, tiled=True)
 
+    mixed_shape, block_shape = (RANKS, 2, CHANS, SLICE), (RANKS, CHANS, SLICE)
     slices = jnp.transpose(output_gradient.reshape(CHANS, RANKS, SLICE), (1, 0, 2))
     samples = exchange(slices, "ctx")
     filters = by_frequency(filter_spectrum)
     saved = by_frequency(input_spectrum[0])
-    mixed = call(spread_kernel, [pltpu.VMEM((RANKS, 2, CHANS, SLICE), jnp.float32)], [VMEM])(on_chip(samples))
+    mixed = call(spread_kernel, [pltpu.HBM(mixed_shape, jnp.float32)], [VMEM], leaving(mixed_shape, TILES))(on_chip(samples))
     mixed = exchange(mixed, "ctx")
     work = (ROWS, CHANS, 2 * LANES)
     scratch = [pltpu.VMEM(work, jnp.float32), pltpu.VMEM((2, ROWS, LANES), jnp.float32)]
@@ -310,13 +327,14 @@
     total = sum_over_sequences(keep, send, owners)
     parts = call(
         inverse_kernel,
-        [pltpu.VMEM((RANKS, 2, CHANS, SLICE), jnp.float32)],
+        [pltpu.VMEM(mixed_shape, jnp.float32)],
         [VMEM] * 7,
         scratch,
     )(on_chip(spectrum), on_chip(filters), scalars, shift, middle, *back)
     parts = exchange(parts, "ctx")
-    blocks = call(gather_kernel, [pltpu.VMEM((RANKS, CHANS, SLICE), jnp.float32)], [VMEM])(on_chip(parts))
+    blocks = call(gather_kernel, [pltpu.HBM(block_shape, jnp.float32)], [VMEM], leaving(block_shape, TILES))(on_chip(parts))
     blocks = exchange(blocks, "ctx")
+    blocks = blocks * (1.0 / LENGTH)
     input_gradient = jnp.transpose(blocks, (1, 0, 2)).reshape(1, CHANS, TOKENS)
     total = total.reshape(2, LANES // owners, ROWS, CHANS)
     filter_gradient = jnp.transpose(total, (3, 0, 1, 2)).reshape(CHANS, 2, TOKENS // owners)

time: 100 us -> 97.6 us (0.976)
  the two profiles are of different devices: /device:TPU:10 before, /device:TPU:2 now
where the time goes in v4:
time: 97.6 us; the launch traced here: 96.9 us
  starting transfers between devices  47 us (48%)
  blocking collectives  24.3 us (25%)
  waiting for transfers between devices  15 us (15%)
  local copies, waits for them, and re-layouts  4.96 us (5%)
  Pallas kernels  3.97 us (4%)
    all_to_all x1, blocking collectives, per_device(): lax.all_to_all(array, axis, split_axis=0, concat_axis=0, tiled=True)  24.3 us
    all_to_all x3, starting transfers between devices, per_device(): lax.all_to_all(array, axis, split_axis=0, concat_axis=0, tiled=True)  23.5 us
    ppermute x7, starting transfers between devices, swap(): return lax.ppermute(array, 'dp', [(i, i ^ apart) for i in range(owners)])  23.5 us
    all_to_all x3, waiting for transfers between devices, per_device(): lax.all_to_all(array, axis, split_axis=0, concat_axis=0, tiled=True)  10.2 us
    ppermute x7, waiting for transfers between devices, swap(): return lax.ppermute(array, 'dp', [(i, i ^ apart) for i in range(owners)])  4.82 us
  transfers between devices with their start and end apart: 10, of which 4 were waited for; matrix products, arithmetic and copies ran while one was open for 5% of the time, Pallas kernels for 1%

profile of v4, /device:TPU:2, one launch (start us, length us, event | category | flops | bytes accessed | tf_op | source)
XLA Modules:
  0.0 96.9 jit_solution(286297040392469549)
XLA Ops:
  0.6 24.3 %all_to_all.20.samples_ref = f32[16,8,512]{2,1,0:T(8,128)S(1)} all-to-all(f32[16,8,512]{2,1,0:T(8,128)} %bitcast.45), channel_id=1, replica_groups=mesh['dp'=32,'ctx'=16] {'ctx'}, dimensions={0} | all-to-all | bytes 524288 | tf_op jit(solution)/shard_map/all_to_all | solution.py:305
  24.9 0.9 shard_map.113
  25.8 5.8 %all-to-all-start.1 = ((f32[16,2,8,512]{3,2,1,0:T(8,128)}), f32[16,2,8,512]{3,2,1,0:T(8,128)S(1)}, u32[]{:S(2)}, u32[]{:S(2)}) async-start(f32[16,2,8,512]{3,2,1,0:T(8,128)} %shard_map.113), calls=%async_computation.1 | async-start | bytes 1048576 | tf_op jit(solution)/shard_map/all_to_all | solution.py:305
  31.9 0.4 reshape.39
  32.7 0.7 dynamic-slice_bitcast_fusion.shift_ref
  33.4 0.7 dynamic-slice_bitcast_fusion.1
  34.1 10.1 %all-to-all-done.1.mixed_ref = f32[16,2,8,512]{3,2,1,0:T(8,128)S(1)} async-done(((f32[16,2,8,512]{3,2,1,0:T(8,128)}), f32[16,2,8,512]{3,2,1,0:T(8,128)S(1)}, u32[]{:S(2)}, u32[]{:S(2)}) %all-to-all-start.1) | async-done | bytes 524320 | tf_op jit(solution)/shard_map/all_to_all | solution.py:305
  44.4 0.6 shard_map.114.spectrum_ref
  45.4 1.4 %shard_map.115 = f32[16,2,8,512]{3,2,1,0:T(8,128)} custom-call(f32[64,8,256]{2,1,0:T(8,128)S(1)} %shard_map.114.spectrum_ref, f32[64,8,256]{2,1,0:T(8,128)S(1)} %bitcast.40, f32[2,72,128]{2,1,0:T(8,128)S(1)} %broadcast_in_dim.2.scalars_ref, f32[2,128]{1,0:T(2,128)S(1)} %dynamic-slice_bitcast_fusion.shift_ref, f32[2,64,128]{2,1,0:T(8,128)S(1)} %copy-done, ...), custom_call_target="tpu_custom_call" | custom-call | tf_op jit(solution)/shard_map/pallas_call | solution.py:328
  46.8 8.1 %all-to-all-start.2 = ((f32[16,2,8,512]{3,2,1,0:T(8,128)}), f32[16,2,8,512]{3,2,1,0:T(8,128)S(1)}, u32[]{:S(2)}, u32[]{:S(2)}) async-start(f32[16,2,8,512]{3,2,1,0:T(8,128)} %shard_map.115), calls=%async_computation.2 | async-start | bytes 1048576 | tf_op jit(solution)/shard_map/all_to_all | solution.py:305
  56.3 1.9 %collective-permute-start = (f32[16,8,512]{2,1,0:T(8,128)S(1)}, f32[16,8,512]{2,1,0:T(8,128)S(1)}, u32[]{:S(2)}, u32[]{:S(2)}) collective-permute-start(f32[16,8,512]{2,1,0:T(8,128)S(1)} %get-tuple-element.5), channel_id=1, source_target_pairs={{0,16},{16,0},{32,48},{48,32},{64,80},{80,64},{96,112},{112,96},{1... | collective-permute-start | bytes 786440 | tf_op jit(solution)/shard_map/ppermute | solution.py:238
  58.2 1.5 %collective-permute-done = f32[16,8,512]{2,1,0:T(8,128)S(1)} collective-permute-done((f32[16,8,512]{2,1,0:T(8,128)S(1)}, f32[16,8,512]{2,1,0:T(8,128)S(1)}, u32[]{:S(2)}, u32[]{:S(2)}) %collective-permute-start) | collective-permute-done | bytes 262176 | tf_op jit(solution)/shard_map/ppermute | solution.py:238
  59.8 4.5 %collective-permute-start.1 = (f32[4,8,512]{2,1,0:T(8,128)S(1)}, f32[4,8,512]{2,1,0:T(8,128)S(1)}, u32[]{:S(2)}, u32[]{:S(2)}) collective-permute-start(f32[4,8,512]{2,1,0:T(8,128)S(1)} %get-tuple-element.8), channel_id=1, source_target_pairs={{0,64},{16,80},{32,96},{48,112},{64,0},{80,16},{96,32},{112,48},{1... | collective-permute-start | bytes 196616 | tf_op jit(solution)/shard_map/ppermute | solution.py:238
  64.3 5.7 %collective-permute-start.3 = (f32[4,8,512]{2,1,0:T(8,128)S(1)}, f32[4,8,512]{2,1,0:T(8,128)S(1)}, u32[]{:S(2)}, u32[]{:S(2)}) collective-permute-start(f32[4,8,512]{2,1,0:T(8,128)S(1)} %get-tuple-element.9), channel_id=1, source_target_pairs={{0,192},{16,208},{32,224},{48,240},{64,128},{80,144},{96,160},{112... | collective-permute-start | bytes 196616 | tf_op jit(solution)/shard_map/ppermute | solution.py:238
  70.0 2.2 %collective-permute-start.2 = (f32[4,8,512]{2,1,0:T(8,128)S(1)}, f32[4,8,512]{2,1,0:T(8,128)S(1)}, u32[]{:S(2)}, u32[]{:S(2)}) collective-permute-start(f32[4,8,512]{2,1,0:T(8,128)S(1)} %get-tuple-element.10), channel_id=1, source_target_pairs={{0,128},{16,144},{32,160},{48,176},{64,192},{80,208},{96,224},{112... | collective-permute-start | bytes 196616 | tf_op jit(solution)/shard_map/ppermute | solution.py:238
  72.2 0.8 shard_map.116
  73.0 9.6 %all-to-all-start.3 = ((f32[16,8,512]{2,1,0:T(8,128)}), f32[16,8,512]{2,1,0:T(8,128)S(1)}, u32[]{:S(2)}, u32[]{:S(2)}) async-start(f32[16,8,512]{2,1,0:T(8,128)} %shard_map.116), calls=%async_computation.3 | async-start | bytes 524288 | tf_op jit(solution)/shard_map/all_to_all | solution.py:305
  82.7 3.4 %collective-permute-start.4 = (f32[8,512]{1,0:T(8,128)S(1)}, f32[8,512]{1,0:T(8,128)S(1)}, u32[]{:S(2)}, u32[]{:S(2)}) collective-permute-start(f32[8,512]{1,0:T(8,128)S(1)} %get-tuple-element.11), channel_id=1, source_target_pairs={{0,32},{16,48},{32,0},{48,16},{64,96},{80,112},{96,64},{112,80},{1... | collective-permute-start | bytes 49160 | tf_op jit(solution)/shard_map/ppermute | solution.py:238
  86.1 3.6 %collective-permute-start.6 = (f32[8,512]{1,0:T(8,128)S(1)}, f32[8,512]{1,0:T(8,128)S(1)}, u32[]{:S(2)}, u32[]{:S(2)}) collective-permute-start(f32[8,512]{1,0:T(8,128)S(1)} %get-tuple-element.12), channel_id=1, source_target_pairs={{0,288},{16,304},{32,256},{48,272},{64,352},{80,368},{96,320},{112... | collective-permute-start | bytes 49160 | tf_op jit(solution)/shard_map/ppermute | solution.py:238
  89.6 2.3 %collective-permute-start.5 = (f32[8,512]{1,0:T(8,128)S(1)}, f32[8,512]{1,0:T(8,128)S(1)}, u32[]{:S(2)}, u32[]{:S(2)}) collective-permute-start(f32[8,512]{1,0:T(8,128)S(1)} %get-tuple-element.13), channel_id=1, source_target_pairs={{0,256},{16,272},{32,288},{48,304},{64,320},{80,336},{96,352},{112... | collective-permute-start | bytes 49160 | tf_op jit(solution)/shard_map/ppermute | solution.py:238
  92.0 0.6 collective-permute-done.6
  92.6 2.7 %collective-permute-done.5 = f32[8,512]{1,0:T(8,128)S(1)} collective-permute-done((f32[8,512]{1,0:T(8,128)S(1)}, f32[8,512]{1,0:T(8,128)S(1)}, u32[]{:S(2)}, u32[]{:S(2)}) %collective-permute-start.5) | collective-permute-done | bytes 16416 | tf_op jit(solution)/shard_map/ppermute | solution.py:238
  95.4 0.7 copy.19
  96.2 0.7 broadcast_multiply_fusion
  (33 shorter events, 2.8 us)
Async XLA Ops:
  25.8 5.8 %copy-start.5 = (f32[8,2,8192]{2,1,0:T(2,128)S(1)}, f32[8,2,8192]{2,1,0:T(2,128)}, u32[]{:S(2)}) copy-start(f32[8,2,8192]{2,1,0:T(2,128)} %param.12) | copy-start | bytes 1572868
  25.8 18.5 %all-to-all-start.1 = ((f32[16,2,8,512]{3,2,1,0:T(8,128)}), f32[16,2,8,512]{3,2,1,0:T(8,128)S(1)}, u32[]{:S(2)}, u32[]{:S(2)}) async-start(f32[16,2,8,512]{3,2,1,0:T(8,128)} %shard_map.113), calls=%async_computation.1 | async-start | bytes 1048576 | tf_op jit(solution)/shard_map/all_to_all | solution.py:305
  32.3 12.1 %copy-start.3 = (bf16[256,256]{1,0:T(8,128)(2,1)S(1)}, bf16[256,256]{1,0:T(8,128)(2,1)}, u32[]{:S(2)}) copy-start(bf16[256,256]{1,0:T(8,128)(2,1)} %constant.39.clone.low_ref) | copy-start | bytes 393220
  32.3 12.1 %copy-start.4 = (bf16[256,256]{1,0:T(8,128)(2,1)S(1)}, bf16[256,256]{1,0:T(8,128)(2,1)}, u32[]{:S(2)}) copy-start(bf16[256,256]{1,0:T(8,128)(2,1)} %constant.38.clone.high_ref) | copy-start | bytes 393220
  32.7 11.7 %copy-start = (f32[2,64,128]{2,1,0:T(8,128)S(1)}, f32[2,64,128]{2,1,0:T(8,128)}, u32[]{:S(2)}) copy-start(f32[2,64,128]{2,1,0:T(8,128)} %constant.37.clone.middle_ref) | copy-start | bytes 196612
  44.4 0.9 copy-start.1
  44.4 1.0 copy-start.2
  46.8 8.1 %copy-start.6 = (f32[1,8,2,8192]{3,2,1,0:T(2,128)S(1)}, f32[1,8,2,8192]{3,2,1,0:T(2,128)}, u32[]{:S(2)}) copy-start(f32[1,8,2,8192]{3,2,1,0:T(2,128)} %param.11) | copy-start | bytes 1572868
  46.8 25.4 %all-to-all-start.2 = ((f32[16,2,8,512]{3,2,1,0:T(8,128)}), f32[16,2,8,512]{3,2,1,0:T(8,128)S(1)}, u32[]{:S(2)}, u32[]{:S(2)}) async-start(f32[16,2,8,512]{3,2,1,0:T(8,128)} %shard_map.115), calls=%async_computation.2 | async-start | bytes 1048576 | tf_op jit(solution)/shard_map/all_to_all | solution.py:305
  56.3 3.4 %collective-permute-start = (f32[16,8,512]{2,1,0:T(8,128)S(1)}, f32[16,8,512]{2,1,0:T(8,128)S(1)}, u32[]{:S(2)}, u32[]{:S(2)}) collective-permute-start(f32[16,8,512]{2,1,0:T(8,128)S(1)} %get-tuple-element.5), channel_id=1, source_target_pairs={{0,16},{16,0},{32,48},{48,32},{64,80},{80,64},{96,112},{112,96},{1... | collective-permute-start | bytes 786440 | tf_op jit(solution)/shard_map/ppermute | solution.py:238
  59.8 22.9 %collective-permute-start.1 = (f32[4,8,512]{2,1,0:T(8,128)S(1)}, f32[4,8,512]{2,1,0:T(8,128)S(1)}, u32[]{:S(2)}, u32[]{:S(2)}) collective-permute-start(f32[4,8,512]{2,1,0:T(8,128)S(1)} %get-tuple-element.8), channel_id=1, source_target_pairs={{0,64},{16,80},{32,96},{48,112},{64,0},{80,16},{96,32},{112,48},{1... | collective-permute-start | bytes 196616 | tf_op jit(solution)/shard_map/ppermute | solution.py:238
  64.3 18.4 %collective-permute-start.3 = (f32[4,8,512]{2,1,0:T(8,128)S(1)}, f32[4,8,512]{2,1,0:T(8,128)S(1)}, u32[]{:S(2)}, u32[]{:S(2)}) collective-permute-start(f32[4,8,512]{2,1,0:T(8,128)S(1)} %get-tuple-element.9), channel_id=1, source_target_pairs={{0,192},{16,208},{32,224},{48,240},{64,128},{80,144},{96,160},{112... | collective-permute-start | bytes 196616 | tf_op jit(solution)/shard_map/ppermute | solution.py:238
  70.0 12.7 %collective-permute-start.2 = (f32[4,8,512]{2,1,0:T(8,128)S(1)}, f32[4,8,512]{2,1,0:T(8,128)S(1)}, u32[]{:S(2)}, u32[]{:S(2)}) collective-permute-start(f32[4,8,512]{2,1,0:T(8,128)S(1)} %get-tuple-element.10), channel_id=1, source_target_pairs={{0,128},{16,144},{32,160},{48,176},{64,192},{80,208},{96,224},{112... | collective-permute-start | bytes 196616 | tf_op jit(solution)/shard_map/ppermute | solution.py:238
  73.0 23.2 %all-to-all-start.3 = ((f32[16,8,512]{2,1,0:T(8,128)}), f32[16,8,512]{2,1,0:T(8,128)S(1)}, u32[]{:S(2)}, u32[]{:S(2)}) async-start(f32[16,8,512]{2,1,0:T(8,128)} %shard_map.116), calls=%async_computation.3 | async-start | bytes 524288 | tf_op jit(solution)/shard_map/all_to_all | solution.py:305
  82.7 9.2 %collective-permute-start.4 = (f32[8,512]{1,0:T(8,128)S(1)}, f32[8,512]{1,0:T(8,128)S(1)}, u32[]{:S(2)}, u32[]{:S(2)}) collective-permute-start(f32[8,512]{1,0:T(8,128)S(1)} %get-tuple-element.11), channel_id=1, source_target_pairs={{0,32},{16,48},{32,0},{48,16},{64,96},{80,112},{96,64},{112,80},{1... | collective-permute-start | bytes 49160 | tf_op jit(solution)/shard_map/ppermute | solution.py:238
  86.1 6.5 %collective-permute-start.6 = (f32[8,512]{1,0:T(8,128)S(1)}, f32[8,512]{1,0:T(8,128)S(1)}, u32[]{:S(2)}, u32[]{:S(2)}) collective-permute-start(f32[8,512]{1,0:T(8,128)S(1)} %get-tuple-element.12), channel_id=1, source_target_pairs={{0,288},{16,304},{32,256},{48,272},{64,352},{80,368},{96,320},{112... | collective-permute-start | bytes 49160 | tf_op jit(solution)/shard_map/ppermute | solution.py:238
  89.6 5.6 %collective-permute-start.5 = (f32[8,512]{1,0:T(8,128)S(1)}, f32[8,512]{1,0:T(8,128)S(1)}, u32[]{:S(2)}, u32[]{:S(2)}) collective-permute-start(f32[8,512]{1,0:T(8,128)S(1)} %get-tuple-element.13), channel_id=1, source_target_pairs={{0,256},{16,272},{32,288},{48,304},{64,320},{80,336},{96,352},{112... | collective-permute-start | bytes 49160 | tf_op jit(solution)/shard_map/ppermute | solution.py:238

commit v5 on v4

--- a/solution.py
+++ b/solution.py
@@ -180,7 +180,8 @@
 
 
 def inverse_kernel(
-    spectrum_ref, filter_ref, scalars_ref, shift_ref, middle_ref, high_ref, low_ref, out_ref, work_ref, twiddle_ref
+    spectrum_ref, filter_ref, scalars_ref, shift_ref, middle_ref, high_ref, low_ref, sent_ref, work_ref, twiddle_ref,
+    out_ref, semaphores,
 ):
     twiddles(shift_ref, middle_ref, twiddle_ref)
 
@@ -200,13 +201,20 @@
         for inner in range(8):
             value = values[inner]
             store(work_ref, 8 * inner + a, times(value, scalar(8 + 8 * inner + a)) if inner else value)
+    copies = []
     for inner in range(8):
         values = dft8([load(work_ref, 8 * inner + a) for a in range(8)], 1)
         for outer in range(8):
             real, imag = times(values[outer], scalar(outer)) if outer else values[outer]
-            rank, lanes = source(8 * outer + inner)
-            out_ref[rank, 0, :, lanes] = real
-            out_ref[rank, 1, :, lanes] = imag
+            lanes = slice(inner % TILES * LANES, (inner % TILES + 1) * LANES)
+            out_ref[outer, inner // TILES, 0, :, lanes] = real
+            out_ref[outer, inner // TILES, 1, :, lanes] = imag
+        if inner % TILES == TILES - 1:
+            half = inner // TILES
+            copies.append(pltpu.make_async_copy(out_ref.at[:, half], sent_ref.at[:, half], semaphores.at[half]))
+            copies[-1].start()
+    for copy in copies:
+        copy.wait()
 
 
 def term_kernel(rank_ref, spectrum_ref, saved_ref, keep_ref, send_ref):
@@ -216,15 +224,17 @@
     saved = saved_ref[...].reshape(ROWS * CHANS, 2 * LANES)
     term = times((spectrum[:, :LANES], spectrum[:, LANES:]), (saved[:, :LANES], -saved[:, LANES:]))
     turned = [part.T for part in term]
+    side = rank >> 1 & 1
     for pair in range(owners // 2):
-        apart = rank >> 1 ^ pair
-        slot = (apart >> 1 & 3) << 2 | apart >> 3 << 1 | apart & 1
+        first = pair >> 1 << 2 | pair & 1
+        apart = (rank ^ first) & ~2
+        slot = (apart >> 2 & 3) << 2 | apart >> 4 << 1 | apart & 1
         for part in range(2):
             place = slice(part * rows, (part + 1) * rows)
-            even = turned[part][2 * pair * rows : (2 * pair + 1) * rows, :]
-            odd = turned[part][(2 * pair + 1) * rows : (2 * pair + 2) * rows, :]
-            keep_ref[slot, place, :] = jnp.where(rank & 1 == 0, even, odd)
-            send_ref[slot, place, :] = jnp.where(rank & 1 == 0, odd, even)
+            even = turned[part][first * rows : (first + 1) * rows, :]
+            odd = turned[part][(first + 2) * rows : (first + 3) * rows, :]
+            keep_ref[slot, place, :] = jnp.where(side == 0, even, odd)
+            send_ref[slot, place, :] = jnp.where(side == 0, odd, even)
 
 
 def summed(total, sent):
@@ -237,10 +247,10 @@
     def swap(array, apart):
         return lax.ppermute(array, "dp", [(i, i ^ apart) for i in range(owners)])
 
-    total = keep + swap(send, 1)
+    total = keep + swap(send, 2)
     total = total.reshape(4, 4, *keep.shape[1:])
     total = summed(total[0], [swap(total[k], (0, 4, 8, 12)[k]) for k in range(1, 4)])
-    return summed(total[0], [swap(total[k], (0, 2, 16, 18)[k]) for k in range(1, 4)])
+    return summed(total[0], [swap(total[k], (0, 1, 16, 17)[k]) for k in range(1, 4)])
 
 
 def call(kernel, outs, in_specs, scratch=()):
@@ -304,6 +314,7 @@
     own = lambda table: lax.dynamic_index_in_dim(jnp.asarray(table), rank, 0, keepdims=False)
     exchange = lambda array, axis: lax.all_to_all(array, axis, split_axis=0, concat_axis=0, tiled=True)
 
+    half_shape = (RANKS // 2, 2, 2, CHANS, SLICE)
     mixed_shape, block_shape = (RANKS, 2, CHANS, SLICE), (RANKS, CHANS, SLICE)
     slices = jnp.transpose(output_gradient.reshape(CHANS, RANKS, SLICE), (1, 0, 2))
     samples = exchange(slices, "ctx")
@@ -327,10 +338,10 @@
     total = sum_over_sequences(keep, send, owners)
     parts = call(
         inverse_kernel,
-        [pltpu.VMEM(mixed_shape, jnp.float32)],
+        [pltpu.HBM(half_shape, jnp.float32)],
         [VMEM] * 7,
-        scratch,
-    )(on_chip(spectrum), on_chip(filters), scalars, shift, middle, *back)
+        scratch + leaving(half_shape, 2),
+    )(on_chip(spectrum), on_chip(filters), scalars, shift, middle, *back).reshape(mixed_shape)
     parts = exchange(parts, "ctx")
     blocks = call(gather_kernel, [pltpu.HBM(block_shape, jnp.float32)], [VMEM], leaving(block_shape, TILES))(on_chip(parts))
     blocks = exchange(blocks, "ctx")

time: 97.6 us -> 102 us (1.045)
  waiting for transfers between devices: 15 us -> 18.6 us
    ppermute x7, waiting for transfers between devices: 4.82 us -> 8.47 us  [swap(): return lax.ppermute(array, 'dp', [(i, i ^ apart) for i in range(owners)])]
  transfers between devices with their start and end apart: 10 -> 10, of which waited for: 4 -> 3; matrix products, arithmetic and copies ran while one was open for 5% -> 5% of each run, Pallas kernels for 1% -> 1%
where the time goes in v5:
time: 102 us
  starting transfers between devices  48 us (47%)
  blocking collectives  24.3 us (24%)
  waiting for transfers between devices  18.6 us (18%)
  local copies, waits for them, and re-layouts  4.97 us (5%)
  Pallas kernels  3.97 us (4%)
    ppermute x7, starting transfers between devices, swap(): return lax.ppermute(array, 'dp', [(i, i ^ apart) for i in range(owners)])  24.5 us
    all_to_all x1, blocking collectives, per_device(): lax.all_to_all(array, axis, split_axis=0, concat_axis=0, tiled=True)  24.3 us
    all_to_all x3, starting transfers between devices, per_device(): lax.all_to_all(array, axis, split_axis=0, concat_axis=0, tiled=True)  23.5 us
    all_to_all x3, waiting for transfers between devices, per_device(): lax.all_to_all(array, axis, split_axis=0, concat_axis=0, tiled=True)  10.2 us
    ppermute x7, waiting for transfers between devices, swap(): return lax.ppermute(array, 'dp', [(i, i ^ apart) for i in range(owners)])  8.47 us
  transfers between devices with their start and end apart: 10, of which 3 were waited for; matrix products, arithmetic and copies ran while one was open for 5% of the time, Pallas kernels for 1%

profile of v5, /device:TPU:2, one launch (start us, length us, event | category | flops | bytes accessed | tf_op | source)
XLA Modules:
  0.0 101.5 jit_solution(14308800244016186494)
XLA Ops:
  0.6 24.3 %all_to_all.20.samples_ref = f32[16,8,512]{2,1,0:T(8,128)S(1)} all-to-all(f32[16,8,512]{2,1,0:T(8,128)} %bitcast.47), channel_id=1, replica_groups=mesh['dp'=32,'ctx'=16] {'ctx'}, dimensions={0} | all-to-all | bytes 524288 | tf_op jit(solution)/shard_map/all_to_all | solution.py:315
  24.9 0.9 shard_map.113
  25.8 5.8 %all-to-all-start.1 = ((f32[16,2,8,512]{3,2,1,0:T(8,128)}), f32[16,2,8,512]{3,2,1,0:T(8,128)S(1)}, u32[]{:S(2)}, u32[]{:S(2)}) async-start(f32[16,2,8,512]{3,2,1,0:T(8,128)} %shard_map.113), calls=%async_computation.1 | async-start | bytes 1048576 | tf_op jit(solution)/shard_map/all_to_all | solution.py:315
  31.9 0.4 reshape.42
  32.7 0.7 dynamic-slice_bitcast_fusion.shift_ref
  33.4 0.7 dynamic-slice_bitcast_fusion.1
  34.1 10.1 %all-to-all-done.1.mixed_ref = f32[16,2,8,512]{3,2,1,0:T(8,128)S(1)} async-done(((f32[16,2,8,512]{3,2,1,0:T(8,128)}), f32[16,2,8,512]{3,2,1,0:T(8,128)S(1)}, u32[]{:S(2)}, u32[]{:S(2)}) %all-to-all-start.1) | async-done | bytes 524320 | tf_op jit(solution)/shard_map/all_to_all | solution.py:315
  44.4 0.6 shard_map.114.spectrum_ref
  45.4 1.4 %shard_map.115 = f32[8,2,2,8,512]{4,3,2,1,0:T(8,128)} custom-call(f32[64,8,256]{2,1,0:T(8,128)S(1)} %shard_map.114.spectrum_ref, f32[64,8,256]{2,1,0:T(8,128)S(1)} %bitcast.41, f32[2,72,128]{2,1,0:T(8,128)S(1)} %broadcast_in_dim.2.scalars_ref, f32[2,128]{1,0:T(2,128)S(1)} %dynamic-slice_bitcast_fusion.shift_ref, f32[2,64,128]{2,1,0:T(8,128)S(1)} %copy-done, ...), custom_call_target="tpu_custom_call" | custom-call | tf_op jit(solution)/shard_map/pallas_call | solution.py:339
  46.8 8.1 %all-to-all-start.2 = ((f32[16,2,8,512]{3,2,1,0:T(8,128)}), f32[16,2,8,512]{3,2,1,0:T(8,128)S(1)}, u32[]{:S(2)}, u32[]{:S(2)}) async-start(f32[16,2,8,512]{3,2,1,0:T(8,128)} %bitcast.45), calls=%async_computation.2 | async-start | bytes 1048576 | tf_op jit(solution)/shard_map/all_to_all | solution.py:315
  55.2 0.4 reshape_squeeze.3
  56.3 3.5 %collective-permute-start = (f32[16,8,512]{2,1,0:T(8,128)S(1)}, f32[16,8,512]{2,1,0:T(8,128)S(1)}, u32[]{:S(2)}, u32[]{:S(2)}) collective-permute-start(f32[16,8,512]{2,1,0:T(8,128)S(1)} %get-tuple-element.5), channel_id=1, source_target_pairs={{0,32},{16,48},{32,0},{48,16},{64,96},{80,112},{96,64},{112,80},{1... | collective-permute-start | bytes 786440 | tf_op jit(solution)/shard_map/ppermute | solution.py:248
  59.8 4.8 %collective-permute-done = f32[16,8,512]{2,1,0:T(8,128)S(1)} collective-permute-done((f32[16,8,512]{2,1,0:T(8,128)S(1)}, f32[16,8,512]{2,1,0:T(8,128)S(1)}, u32[]{:S(2)}, u32[]{:S(2)}) %collective-permute-start) | collective-permute-done | bytes 262176 | tf_op jit(solution)/shard_map/ppermute | solution.py:248
  64.6 5.2 %collective-permute-start.1 = (f32[4,8,512]{2,1,0:T(8,128)S(1)}, f32[4,8,512]{2,1,0:T(8,128)S(1)}, u32[]{:S(2)}, u32[]{:S(2)}) collective-permute-start(f32[4,8,512]{2,1,0:T(8,128)S(1)} %get-tuple-element.8), channel_id=1, source_target_pairs={{0,64},{16,80},{32,96},{48,112},{64,0},{80,16},{96,32},{112,48},{1... | collective-permute-start | bytes 196616 | tf_op jit(solution)/shard_map/ppermute | solution.py:248
  69.9 5.0 %collective-permute-start.3 = (f32[4,8,512]{2,1,0:T(8,128)S(1)}, f32[4,8,512]{2,1,0:T(8,128)S(1)}, u32[]{:S(2)}, u32[]{:S(2)}) collective-permute-start(f32[4,8,512]{2,1,0:T(8,128)S(1)} %get-tuple-element.9), channel_id=1, source_target_pairs={{0,192},{16,208},{32,224},{48,240},{64,128},{80,144},{96,160},{112... | collective-permute-start | bytes 196616 | tf_op jit(solution)/shard_map/ppermute | solution.py:248
  74.9 2.4 %collective-permute-start.2 = (f32[4,8,512]{2,1,0:T(8,128)S(1)}, f32[4,8,512]{2,1,0:T(8,128)S(1)}, u32[]{:S(2)}, u32[]{:S(2)}) collective-permute-start(f32[4,8,512]{2,1,0:T(8,128)S(1)} %get-tuple-element.10), channel_id=1, source_target_pairs={{0,128},{16,144},{32,160},{48,176},{64,192},{80,208},{96,224},{112... | collective-permute-start | bytes 196616 | tf_op jit(solution)/shard_map/ppermute | solution.py:248
  77.3 0.8 shard_map.116
  78.1 9.6 %all-to-all-start.3 = ((f32[16,8,512]{2,1,0:T(8,128)}), f32[16,8,512]{2,1,0:T(8,128)S(1)}, u32[]{:S(2)}, u32[]{:S(2)}) async-start(f32[16,8,512]{2,1,0:T(8,128)} %shard_map.116), calls=%async_computation.3 | async-start | bytes 524288 | tf_op jit(solution)/shard_map/all_to_all | solution.py:315
  87.8 1.9 %collective-permute-start.4 = (f32[8,512]{1,0:T(8,128)S(1)}, f32[8,512]{1,0:T(8,128)S(1)}, u32[]{:S(2)}, u32[]{:S(2)}) collective-permute-start(f32[8,512]{1,0:T(8,128)S(1)} %get-tuple-element.11), channel_id=1, source_target_pairs={{0,16},{16,0},{32,48},{48,32},{64,80},{80,64},{96,112},{112,96},{1... | collective-permute-start | bytes 49160 | tf_op jit(solution)/shard_map/ppermute | solution.py:248
  89.7 4.6 %collective-permute-start.6 = (f32[8,512]{1,0:T(8,128)S(1)}, f32[8,512]{1,0:T(8,128)S(1)}, u32[]{:S(2)}, u32[]{:S(2)}) collective-permute-start(f32[8,512]{1,0:T(8,128)S(1)} %get-tuple-element.12), channel_id=1, source_target_pairs={{0,272},{16,256},{32,304},{48,288},{64,336},{80,320},{96,368},{112... | collective-permute-start | bytes 49160 | tf_op jit(solution)/shard_map/ppermute | solution.py:248
  94.3 1.9 %collective-permute-start.5 = (f32[8,512]{1,0:T(8,128)S(1)}, f32[8,512]{1,0:T(8,128)S(1)}, u32[]{:S(2)}, u32[]{:S(2)}) collective-permute-start(f32[8,512]{1,0:T(8,128)S(1)} %get-tuple-element.13), channel_id=1, source_target_pairs={{0,256},{16,272},{32,288},{48,304},{64,320},{80,336},{96,352},{112... | collective-permute-start | bytes 49160 | tf_op jit(solution)/shard_map/ppermute | solution.py:248
  96.2 3.7 %collective-permute-done.5 = f32[8,512]{1,0:T(8,128)S(1)} collective-permute-done((f32[8,512]{1,0:T(8,128)S(1)}, f32[8,512]{1,0:T(8,128)S(1)}, u32[]{:S(2)}, u32[]{:S(2)}) %collective-permute-start.5) | collective-permute-done | bytes 16416 | tf_op jit(solution)/shard_map/ppermute | solution.py:248
  100.1 0.7 copy.19
  100.8 0.7 broadcast_multiply_fusion
  (33 shorter events, 2.4 us)
Async XLA Ops:
  25.8 5.8 %copy-start.5 = (f32[8,2,8192]{2,1,0:T(2,128)S(1)}, f32[8,2,8192]{2,1,0:T(2,128)}, u32[]{:S(2)}) copy-start(f32[8,2,8192]{2,1,0:T(2,128)} %param.12) | copy-start | bytes 1572868
  25.8 18.5 %all-to-all-start.1 = ((f32[16,2,8,512]{3,2,1,0:T(8,128)}), f32[16,2,8,512]{3,2,1,0:T(8,128)S(1)}, u32[]{:S(2)}, u32[]{:S(2)}) async-start(f32[16,2,8,512]{3,2,1,0:T(8,128)} %shard_map.113), calls=%async_computation.1 | async-start | bytes 1048576 | tf_op jit(solution)/shard_map/all_to_all | solution.py:315
  32.3 12.1 %copy-start.3 = (bf16[256,256]{1,0:T(8,128)(2,1)S(1)}, bf16[256,256]{1,0:T(8,128)(2,1)}, u32[]{:S(2)}) copy-start(bf16[256,256]{1,0:T(8,128)(2,1)} %constant.39.clone.low_ref) | copy-start | bytes 393220
  32.3 12.1 %copy-start.4 = (bf16[256,256]{1,0:T(8,128)(2,1)S(1)}, bf16[256,256]{1,0:T(8,128)(2,1)}, u32[]{:S(2)}) copy-start(bf16[256,256]{1,0:T(8,128)(2,1)} %constant.38.clone.high_ref) | copy-start | bytes 393220
  32.7 11.7 %copy-start = (f32[2,64,128]{2,1,0:T(8,128)S(1)}, f32[2,64,128]{2,1,0:T(8,128)}, u32[]{:S(2)}) copy-start(f32[2,64,128]{2,1,0:T(8,128)} %constant.37.clone.middle_ref) | copy-start | bytes 196612
  44.4 0.9 copy-start.1
  44.4 1.0 copy-start.2
  46.8 8.1 %copy-start.6 = (f32[1,8,2,8192]{3,2,1,0:T(2,128)S(1)}, f32[1,8,2,8192]{3,2,1,0:T(2,128)}, u32[]{:S(2)}) copy-start(f32[1,8,2,8192]{3,2,1,0:T(2,128)} %param.11) | copy-start | bytes 1572868
  46.8 30.5 %all-to-all-start.2 = ((f32[16,2,8,512]{3,2,1,0:T(8,128)}), f32[16,2,8,512]{3,2,1,0:T(8,128)S(1)}, u32[]{:S(2)}, u32[]{:S(2)}) async-start(f32[16,2,8,512]{3,2,1,0:T(8,128)} %bitcast.45), calls=%async_computation.2 | async-start | bytes 1048576 | tf_op jit(solution)/shard_map/all_to_all | solution.py:315
  56.3 8.3 %collective-permute-start = (f32[16,8,512]{2,1,0:T(8,128)S(1)}, f32[16,8,512]{2,1,0:T(8,128)S(1)}, u32[]{:S(2)}, u32[]{:S(2)}) collective-permute-start(f32[16,8,512]{2,1,0:T(8,128)S(1)} %get-tuple-element.5), channel_id=1, source_target_pairs={{0,32},{16,48},{32,0},{48,16},{64,96},{80,112},{96,64},{112,80},{1... | collective-permute-start | bytes 786440 | tf_op jit(solution)/shard_map/ppermute | solution.py:248
  64.6 23.1 %collective-permute-start.1 = (f32[4,8,512]{2,1,0:T(8,128)S(1)}, f32[4,8,512]{2,1,0:T(8,128)S(1)}, u32[]{:S(2)}, u32[]{:S(2)}) collective-permute-start(f32[4,8,512]{2,1,0:T(8,128)S(1)} %get-tuple-element.8), channel_id=1, source_target_pairs={{0,64},{16,80},{32,96},{48,112},{64,0},{80,16},{96,32},{112,48},{1... | collective-permute-start | bytes 196616 | tf_op jit(solution)/shard_map/ppermute | solution.py:248
  69.9 17.9 %collective-permute-start.3 = (f32[4,8,512]{2,1,0:T(8,128)S(1)}, f32[4,8,512]{2,1,0:T(8,128)S(1)}, u32[]{:S(2)}, u32[]{:S(2)}) collective-permute-start(f32[4,8,512]{2,1,0:T(8,128)S(1)} %get-tuple-element.9), channel_id=1, source_target_pairs={{0,192},{16,208},{32,224},{48,240},{64,128},{80,144},{96,160},{112... | collective-permute-start | bytes 196616 | tf_op jit(solution)/shard_map/ppermute | solution.py:248
  74.9 12.9 %collective-permute-start.2 = (f32[4,8,512]{2,1,0:T(8,128)S(1)}, f32[4,8,512]{2,1,0:T(8,128)S(1)}, u32[]{:S(2)}, u32[]{:S(2)}) collective-permute-start(f32[4,8,512]{2,1,0:T(8,128)S(1)} %get-tuple-element.10), channel_id=1, source_target_pairs={{0,128},{16,144},{32,160},{48,176},{64,192},{80,208},{96,224},{112... | collective-permute-start | bytes 196616 | tf_op jit(solution)/shard_map/ppermute | solution.py:248
  78.1 22.7 %all-to-all-start.3 = ((f32[16,8,512]{2,1,0:T(8,128)}), f32[16,8,512]{2,1,0:T(8,128)S(1)}, u32[]{:S(2)}, u32[]{:S(2)}) async-start(f32[16,8,512]{2,1,0:T(8,128)} %shard_map.116), calls=%async_computation.3 | async-start | bytes 524288 | tf_op jit(solution)/shard_map/all_to_all | solution.py:315
  87.8 8.4 %collective-permute-start.4 = (f32[8,512]{1,0:T(8,128)S(1)}, f32[8,512]{1,0:T(8,128)S(1)}, u32[]{:S(2)}, u32[]{:S(2)}) collective-permute-start(f32[8,512]{1,0:T(8,128)S(1)} %get-tuple-element.11), channel_id=1, source_target_pairs={{0,16},{16,0},{32,48},{48,32},{64,80},{80,64},{96,112},{112,96},{1... | collective-permute-start | bytes 49160 | tf_op jit(solution)/shard_map/ppermute | solution.py:248
  89.7 6.5 %collective-permute-start.6 = (f32[8,512]{1,0:T(8,128)S(1)}, f32[8,512]{1,0:T(8,128)S(1)}, u32[]{:S(2)}, u32[]{:S(2)}) collective-permute-start(f32[8,512]{1,0:T(8,128)S(1)} %get-tuple-element.12), channel_id=1, source_target_pairs={{0,272},{16,256},{32,304},{48,288},{64,336},{80,320},{96,368},{112... | collective-permute-start | bytes 49160 | tf_op jit(solution)/shard_map/ppermute | solution.py:248
  94.3 5.6 %collective-permute-start.5 = (f32[8,512]{1,0:T(8,128)S(1)}, f32[8,512]{1,0:T(8,128)S(1)}, u32[]{:S(2)}, u32[]{:S(2)}) collective-permute-start(f32[8,512]{1,0:T(8,128)S(1)} %get-tuple-element.13), channel_id=1, source_target_pairs={{0,256},{16,272},{32,288},{48,304},{64,320},{80,336},{96,352},{112... | collective-permute-start | bytes 49160 | tf_op jit(solution)/shard_map/ppermute | solution.py:248
